TPU v7x, 256 devices: a whole 4x4x8 slice. The times are simulated.
256 devices in a mesh: gz: 16 (over y, x), gx: 2 (over core), gy: 8 (over z).
Axes of the slice: x: 4, y: 4, z: 8, core: 2. Of those that a mesh axis runs over, the one named last changes fastest.
Arguments:
- conserved: float32 [5, 64, 128, 2048], P(None, 'gz', 'gx', 'gy'), may hold values from -14 to 34, as said below
- residual: float32 [5, 64, 128, 2048], P(None, 'gz', 'gx', 'gy'), may hold values from -6 to 6
Outputs:
- update: float32 [5, 64, 128, 2048], P(None, 'gz', 'gx', 'gy')
Inputs may be any that keep to these rules, and one draw needn't show every extreme that they name: `conserved`: every cell has density between 0.3 and 3 and positive pressure.
All inputs are finite; a program needn't handle non-finite values.
Results may differ from a plain program's by a relative error of at most 0.0003.
Values sent between devices are 32-bit elements; how exact they have to be, the bound alone decides.
A program may use at most 192 MiB of HBM per device.

v0:
```python
import jax
import jax.numpy as jnp
from jax import lax
from jax.sharding import PartitionSpec as P

ADIABATIC = 1.4
COUPLING = 0.7
METRIC = (0.1, 0.1, 1.0)


def shifted(value, axis, steps):
    count = lax.axis_size(axis)
    initial, last = (max(0, -steps), min(count, count - steps))
    return lax.ppermute(value, axis, [(source, source + steps) for source in range(initial, last)])


def with_halo(cells, sides, width):
    for axis, dim in sides:
        count = lax.axis_size(axis)
        ends = count - 1
        head = lax.slice_in_dim(cells, 0, width, axis=dim)
        tail = lax.slice_in_dim(cells, cells.shape[dim] - width, cells.shape[dim], axis=dim)
        cells = jnp.concatenate(
            [
                lax.ppermute(tail, axis, [(i, (i + 1) % count) for i in range(ends)]),
                cells,
                lax.ppermute(head, axis, [((i + 1) % count, i) for i in range(ends)]),
            ],
            axis=dim,
        )
    return cells


def primitives(state_field):
    density = state_field[0]
    velocity = [state_field[1] / density, state_field[2] / density, state_field[3] / density]
    kinetic = (
        0.5
        * density
        * (velocity[0] * velocity[0] + velocity[1] * velocity[1] + velocity[2] * velocity[2])
    )
    pressure = (ADIABATIC - 1.0) * (state_field[4] - kinetic)
    sound = jnp.sqrt(ADIABATIC * pressure / density)
    return (velocity, sound)


def split_jacobian(speed_dir, sound, vector, direction, upwind):
    component = 1 + direction
    radius = jnp.abs(speed_dir) + sound
    eigen = speed_dir + radius if upwind else speed_dir - radius
    zeros = jnp.zeros_like(vector[0])
    parts = [zeros, zeros, zeros, zeros, zeros]
    parts[0] = vector[component]
    parts[component] = vector[0] + vector[4]
    parts[4] = vector[component]
    coupled = jnp.stack(parts)
    return 0.5 * METRIC[direction] * (eigen * vector + COUPLING * sound * coupled)


def diagonal_of(velocity, sound):
    return (
        METRIC[0] * (jnp.abs(velocity[0]) + sound)
        + METRIC[1] * (jnp.abs(velocity[1]) + sound)
        + METRIC[2] * (jnp.abs(velocity[2]) + sound)
    )


def rim_terms(strip, direction):
    density = strip[0]
    guarded = jnp.concatenate([jnp.where(density == 0.0, 1.0, density)[None], strip[1:5]], axis=0)
    velocity, sound = primitives(guarded)
    guess = strip[5:]
    plus = split_jacobian(velocity[direction], sound, guess, direction, True)
    minus = split_jacobian(velocity[direction], sound, guess, direction, False)
    return (plus, minus)


def lower_planes(base, diagonal, speed, sound, incoming):
    carry = incoming
    stars = []
    for height in range(diagonal.shape[0]):
        star = (base[:, height] + carry) / diagonal[height]
        carry = split_jacobian(speed[height], sound[height], star, 2, True)
        stars.append(star)
    return (jnp.stack(stars, axis=1), carry)


def upper_planes(top, diagonal, speed, sound, incoming):
    carry = incoming
    depth = diagonal.shape[0]
    values = [None] * depth
    for height in reversed(range(depth)):
        value = top[:, height] - carry / diagonal[height]
        carry = split_jacobian(speed[height], sound[height], value, 2, False)
        values[height] = value
    return (jnp.stack(values, axis=1), carry)


def wavefront(inputs, local_fn, position, blocks, sender):
    sections = lax.axis_size("gz")
    width = inputs[0].shape[2] // blocks
    columns = inputs[0].shape[3]
    result_init = jnp.zeros(inputs[0].shape, jnp.float32)
    inbox_init = jnp.zeros((5, width, columns), jnp.float32)

    def advance(segment, carry):
        result, inbox = carry
        block = segment - position
        active = jnp.logical_and(block >= 0, block < blocks)
        start = jnp.clip(block, 0, blocks - 1) * width

        def compute(current):
            pieces = [item for item in inputs]
            values, outgoing = local_fn(pieces, inbox)
            return (lax.dynamic_update_slice_in_dim(current, values, start, axis=2), outgoing)

        def remain(current):
            return (current, jnp.zeros_like(inbox))

        result, outgoing = lax.cond(active, compute, remain, result)
        return (result, sender(outgoing))

    final, unused = lax.fori_loop(0, sections + blocks - 1, advance, (result_init, inbox_init))
    return final


def send_above(outgoing):
    return shifted(outgoing, "gz", 1)


def send_below(outgoing):
    return shifted(outgoing, "gz", -1)


def lower_local(pieces, inbox):
    return lower_planes(pieces[0], pieces[1], pieces[2], pieces[3], inbox)


def upper_local(pieces, inbox):
    return upper_planes(pieces[0], pieces[1], pieces[2], pieces[3], inbox)


def per_device(conserved, residual):
    velocity, sound = primitives(conserved)
    diagonal = diagonal_of(velocity, sound)
    predictor = -residual / diagonal
    rows = conserved.shape[2]
    columns = conserved.shape[3]
    joined = jnp.concatenate([conserved, predictor], axis=0)
    padded = with_halo(joined, (("gx", 2), ("gy", 3)), 1)
    plus_x, minus_x = rim_terms(padded[:, :, :, 1 : columns + 1], 0)
    plus_y, minus_y = rim_terms(padded[:, :, 1 : rows + 1, :], 1)
    lower_x = plus_x[:, :, :rows]
    lower_y = plus_y[:, :, :, :columns]
    base = -residual + lower_x + lower_y
    upper_side = minus_x[:, :, 2:] + minus_y[:, :, :, 2:]
    speed = velocity[2]
    blocks = 1
    star_field = wavefront(
        (base, diagonal, speed, sound), lower_local, lax.axis_index("gz"), blocks, send_above
    )
    top = star_field - upper_side / diagonal
    update = wavefront(
        (top, diagonal, speed, sound),
        upper_local,
        lax.axis_size("gz") - 1 - lax.axis_index("gz"),
        blocks,
        send_below,
    )
    return update


def solution(mesh):
    placed = (P(None, "gz", "gx", "gy"), P(None, "gz", "gx", "gy"))
    return jax.shard_map(
        per_device, mesh=mesh, in_specs=placed, out_specs=P(None, "gz", "gx", "gy"), check_vma=False
    )
```

profile of v0, /device:TPU:118, one launch (start us, length us, event | category | flops | bytes accessed | tf_op | source)
XLA Modules:
  0.0 459.8 jit_solution(11775120397687659246)
XLA Ops:
  20.1 5.1 %collective-permute-start.4 = (f32[10,4,66,1]{2,1,3,0:T(4,128)S(1)}, f32[10,4,66,1]{2,1,3,0:T(4,128)}, u32[]{:S(2)}, u32[]{:S(2)}) collective-permute-start(f32[10,4,66,1]{2,1,3,0:T(4,128)S(1)} %copy.39), channel_id=1, source_target_pairs={{0,1},{1,2},{2,3},{3,4},{4,5},{5,6},{6,7},{8,9},{9,10},{10,11},{11... | collective-permute-start | bytes 31688 | tf_op jit(solution)/shard_map/ppermute | solution.py:25
  38.6 6.6 %pad_maximum_fusion.2 = f32[10,4,66,258]{3,1,2,0:T(4,128)S(1)} fusion(f32[10,4,66,1]{3,1,2,0:T(4,128)S(1)} %copy-done, f32[10,4,1,256]{3,1,2,0:T(4,128)S(1)} %collective-permute-done.3, f32[5,4,64,256]{3,1,2,0:T(4,128)S(1)} %fusion.38, f32[5,4,64,256]{3,1,2,0:T(4,128)S(1)} %copy.38, f32[10,4,1,256]{3,1,2,0:T(4,128)S(1)} %collective-permute-done.2, ...), kind=kLoop, calls=%fused_computation.81 | loop fusion | flops 3405600 | bytes 5448960 | tf_op jit(solution)/shard_map/concatenate | solution.py:23
  56.7 195.7 %while.36 = (s32[]{:T(128)}, f32[5,4,64,256]{3,2,0,1:T(8,128)}, f32[5,64,256]{2,1,0:T(8,128)S(1)}, s32[]{:T(128)}, f32[5,4,64,256]{3,2,1,0:T(8,128)S(1)}, /*inde...) while((s32[]{:T(128)}, f32[5,4,64,256]{3,2,0,1:T(8,128)}, ...), condition=%wide.region_3.4_spmd, body=%wide.region_0.3_spmd.sunk | while | flops 4259847 | bytes 12715819 | solution.py:123
  60.1 8.4 %collective-permute-done = f32[5,64,256]{2,1,0:T(8,128)S(1)} collective-permute-done((f32[5,64,256]{2,1,0:T(8,128)S(1)}, f32[5,64,256]{2,1,0:T(8,128)S(1)}, u32[]{:S(2)}, u32[]{:S(2)}) %collective-permute-start) | collective-permute-done | bytes 327712 | tf_op jit(solution)/shard_map/while/body/eval_jaxpr/ppermute | solution.py:14
  68.5 5.2 %collective-permute-start = (f32[5,64,256]{2,1,0:T(8,128)S(1)}, f32[5,64,256]{2,1,0:T(8,128)S(1)}, u32[]{:S(2)}, u32[]{:S(2)}) collective-permute-start(f32[5,64,256]{2,1,0:T(8,128)S(1)} %get-tuple-element.577), channel_id=1, source_target_pairs={{0,16},{16,32},{32,48},{48,64},{64,80},{80,96},{96,112},{112,128},... | collective-permute-start | bytes 983048 | tf_op jit(solution)/shard_map/while/body/eval_jaxpr/ppermute | solution.py:14
  73.7 6.2 %collective-permute-done = f32[5,64,256]{2,1,0:T(8,128)S(1)} collective-permute-done((f32[5,64,256]{2,1,0:T(8,128)S(1)}, f32[5,64,256]{2,1,0:T(8,128)S(1)}, u32[]{:S(2)}, u32[]{:S(2)}) %collective-permute-start) | collective-permute-done | bytes 327712 | tf_op jit(solution)/shard_map/while/body/eval_jaxpr/ppermute | solution.py:14
  80.0 6.5 %collective-permute-start = (f32[5,64,256]{2,1,0:T(8,128)S(1)}, f32[5,64,256]{2,1,0:T(8,128)S(1)}, u32[]{:S(2)}, u32[]{:S(2)}) collective-permute-start(f32[5,64,256]{2,1,0:T(8,128)S(1)} %get-tuple-element.577), channel_id=1, source_target_pairs={{0,16},{16,32},{32,48},{48,64},{64,80},{80,96},{96,112},{112,128},... | collective-permute-start | bytes 983048 | tf_op jit(solution)/shard_map/while/body/eval_jaxpr/ppermute | solution.py:14
  86.5 5.3 %collective-permute-done = f32[5,64,256]{2,1,0:T(8,128)S(1)} collective-permute-done((f32[5,64,256]{2,1,0:T(8,128)S(1)}, f32[5,64,256]{2,1,0:T(8,128)S(1)}, u32[]{:S(2)}, u32[]{:S(2)}) %collective-permute-start) | collective-permute-done | bytes 327712 | tf_op jit(solution)/shard_map/while/body/eval_jaxpr/ppermute | solution.py:14
  91.8 6.5 %collective-permute-start = (f32[5,64,256]{2,1,0:T(8,128)S(1)}, f32[5,64,256]{2,1,0:T(8,128)S(1)}, u32[]{:S(2)}, u32[]{:S(2)}) collective-permute-start(f32[5,64,256]{2,1,0:T(8,128)S(1)} %get-tuple-element.577), channel_id=1, source_target_pairs={{0,16},{16,32},{32,48},{48,64},{64,80},{80,96},{96,112},{112,128},... | collective-permute-start | bytes 983048 | tf_op jit(solution)/shard_map/while/body/eval_jaxpr/ppermute | solution.py:14
  98.3 4.6 collective-permute-done
  103.0 6.5 %collective-permute-start = (f32[5,64,256]{2,1,0:T(8,128)S(1)}, f32[5,64,256]{2,1,0:T(8,128)S(1)}, u32[]{:S(2)}, u32[]{:S(2)}) collective-permute-start(f32[5,64,256]{2,1,0:T(8,128)S(1)} %get-tuple-element.577), channel_id=1, source_target_pairs={{0,16},{16,32},{32,48},{48,64},{64,80},{80,96},{96,112},{112,128},... | collective-permute-start | bytes 983048 | tf_op jit(solution)/shard_map/while/body/eval_jaxpr/ppermute | solution.py:14
  109.5 4.6 collective-permute-done
  114.1 6.5 %collective-permute-start = (f32[5,64,256]{2,1,0:T(8,128)S(1)}, f32[5,64,256]{2,1,0:T(8,128)S(1)}, u32[]{:S(2)}, u32[]{:S(2)}) collective-permute-start(f32[5,64,256]{2,1,0:T(8,128)S(1)} %get-tuple-element.577), channel_id=1, source_target_pairs={{0,16},{16,32},{32,48},{48,64},{64,80},{80,96},{96,112},{112,128},... | collective-permute-start | bytes 983048 | tf_op jit(solution)/shard_map/while/body/eval_jaxpr/ppermute | solution.py:14
  120.6 4.6 collective-permute-done
  125.2 6.5 %collective-permute-start = (f32[5,64,256]{2,1,0:T(8,128)S(1)}, f32[5,64,256]{2,1,0:T(8,128)S(1)}, u32[]{:S(2)}, u32[]{:S(2)}) collective-permute-start(f32[5,64,256]{2,1,0:T(8,128)S(1)} %get-tuple-element.577), channel_id=1, source_target_pairs={{0,16},{16,32},{32,48},{48,64},{64,80},{80,96},{96,112},{112,128},... | collective-permute-start | bytes 983048 | tf_op jit(solution)/shard_map/while/body/eval_jaxpr/ppermute | solution.py:14
  131.7 5.2 %collective-permute-done = f32[5,64,256]{2,1,0:T(8,128)S(1)} collective-permute-done((f32[5,64,256]{2,1,0:T(8,128)S(1)}, f32[5,64,256]{2,1,0:T(8,128)S(1)}, u32[]{:S(2)}, u32[]{:S(2)}) %collective-permute-start) | collective-permute-done | bytes 327712 | tf_op jit(solution)/shard_map/while/body/eval_jaxpr/ppermute | solution.py:14
  136.9 6.5 %collective-permute-start = (f32[5,64,256]{2,1,0:T(8,128)S(1)}, f32[5,64,256]{2,1,0:T(8,128)S(1)}, u32[]{:S(2)}, u32[]{:S(2)}) collective-permute-start(f32[5,64,256]{2,1,0:T(8,128)S(1)} %get-tuple-element.577), channel_id=1, source_target_pairs={{0,16},{16,32},{32,48},{48,64},{64,80},{80,96},{96,112},{112,128},... | collective-permute-start | bytes 983048 | tf_op jit(solution)/shard_map/while/body/eval_jaxpr/ppermute | solution.py:14
  143.4 6.3 %collective-permute-done = f32[5,64,256]{2,1,0:T(8,128)S(1)} collective-permute-done((f32[5,64,256]{2,1,0:T(8,128)S(1)}, f32[5,64,256]{2,1,0:T(8,128)S(1)}, u32[]{:S(2)}, u32[]{:S(2)}) %collective-permute-start) | collective-permute-done | bytes 327712 | tf_op jit(solution)/shard_map/while/body/eval_jaxpr/ppermute | solution.py:14
  149.8 6.5 %collective-permute-start = (f32[5,64,256]{2,1,0:T(8,128)S(1)}, f32[5,64,256]{2,1,0:T(8,128)S(1)}, u32[]{:S(2)}, u32[]{:S(2)}) collective-permute-start(f32[5,64,256]{2,1,0:T(8,128)S(1)} %get-tuple-element.577), channel_id=1, source_target_pairs={{0,16},{16,32},{32,48},{48,64},{64,80},{80,96},{96,112},{112,128},... | collective-permute-start | bytes 983048 | tf_op jit(solution)/shard_map/while/body/eval_jaxpr/ppermute | solution.py:14
  156.3 7.5 %collective-permute-done = f32[5,64,256]{2,1,0:T(8,128)S(1)} collective-permute-done((f32[5,64,256]{2,1,0:T(8,128)S(1)}, f32[5,64,256]{2,1,0:T(8,128)S(1)}, u32[]{:S(2)}, u32[]{:S(2)}) %collective-permute-start) | collective-permute-done | bytes 327712 | tf_op jit(solution)/shard_map/while/body/eval_jaxpr/ppermute | solution.py:14
  163.8 6.5 %collective-permute-start = (f32[5,64,256]{2,1,0:T(8,128)S(1)}, f32[5,64,256]{2,1,0:T(8,128)S(1)}, u32[]{:S(2)}, u32[]{:S(2)}) collective-permute-start(f32[5,64,256]{2,1,0:T(8,128)S(1)} %get-tuple-element.577), channel_id=1, source_target_pairs={{0,16},{16,32},{32,48},{48,64},{64,80},{80,96},{96,112},{112,128},... | collective-permute-start | bytes 983048 | tf_op jit(solution)/shard_map/while/body/eval_jaxpr/ppermute | solution.py:14
  170.3 7.5 %collective-permute-done = f32[5,64,256]{2,1,0:T(8,128)S(1)} collective-permute-done((f32[5,64,256]{2,1,0:T(8,128)S(1)}, f32[5,64,256]{2,1,0:T(8,128)S(1)}, u32[]{:S(2)}, u32[]{:S(2)}) %collective-permute-start) | collective-permute-done | bytes 327712 | tf_op jit(solution)/shard_map/while/body/eval_jaxpr/ppermute | solution.py:14
  177.9 6.5 %collective-permute-start = (f32[5,64,256]{2,1,0:T(8,128)S(1)}, f32[5,64,256]{2,1,0:T(8,128)S(1)}, u32[]{:S(2)}, u32[]{:S(2)}) collective-permute-start(f32[5,64,256]{2,1,0:T(8,128)S(1)} %get-tuple-element.577), channel_id=1, source_target_pairs={{0,16},{16,32},{32,48},{48,64},{64,80},{80,96},{96,112},{112,128},... | collective-permute-start | bytes 983048 | tf_op jit(solution)/shard_map/while/body/eval_jaxpr/ppermute | solution.py:14
  184.4 6.8 %collective-permute-done = f32[5,64,256]{2,1,0:T(8,128)S(1)} collective-permute-done((f32[5,64,256]{2,1,0:T(8,128)S(1)}, f32[5,64,256]{2,1,0:T(8,128)S(1)}, u32[]{:S(2)}, u32[]{:S(2)}) %collective-permute-start) | collective-permute-done | bytes 327712 | tf_op jit(solution)/shard_map/while/body/eval_jaxpr/ppermute | solution.py:14
  197.7 7.8 %collective-permute-done = f32[5,64,256]{2,1,0:T(8,128)S(1)} collective-permute-done((f32[5,64,256]{2,1,0:T(8,128)S(1)}, f32[5,64,256]{2,1,0:T(8,128)S(1)}, u32[]{:S(2)}, u32[]{:S(2)}) %collective-permute-start) | collective-permute-done | bytes 327712 | tf_op jit(solution)/shard_map/while/body/eval_jaxpr/ppermute | solution.py:14
  205.6 8.5 %collective-permute-start = (f32[5,64,256]{2,1,0:T(8,128)S(1)}, f32[5,64,256]{2,1,0:T(8,128)S(1)}, u32[]{:S(2)}, u32[]{:S(2)}) collective-permute-start(f32[5,64,256]{2,1,0:T(8,128)S(1)} %get-tuple-element.577), channel_id=1, source_target_pairs={{0,16},{16,32},{32,48},{48,64},{64,80},{80,96},{96,112},{112,128},... | collective-permute-start | bytes 983048 | tf_op jit(solution)/shard_map/while/body/eval_jaxpr/ppermute | solution.py:14
  214.1 5.0 %collective-permute-done = f32[5,64,256]{2,1,0:T(8,128)S(1)} collective-permute-done((f32[5,64,256]{2,1,0:T(8,128)S(1)}, f32[5,64,256]{2,1,0:T(8,128)S(1)}, u32[]{:S(2)}, u32[]{:S(2)}) %collective-permute-start) | collective-permute-done | bytes 327712 | tf_op jit(solution)/shard_map/while/body/eval_jaxpr/ppermute | solution.py:14
  219.1 6.5 %collective-permute-start = (f32[5,64,256]{2,1,0:T(8,128)S(1)}, f32[5,64,256]{2,1,0:T(8,128)S(1)}, u32[]{:S(2)}, u32[]{:S(2)}) collective-permute-start(f32[5,64,256]{2,1,0:T(8,128)S(1)} %get-tuple-element.577), channel_id=1, source_target_pairs={{0,16},{16,32},{32,48},{48,64},{64,80},{80,96},{96,112},{112,128},... | collective-permute-start | bytes 983048 | tf_op jit(solution)/shard_map/while/body/eval_jaxpr/ppermute | solution.py:14
  225.6 4.6 collective-permute-done
  230.2 6.5 %collective-permute-start = (f32[5,64,256]{2,1,0:T(8,128)S(1)}, f32[5,64,256]{2,1,0:T(8,128)S(1)}, u32[]{:S(2)}, u32[]{:S(2)}) collective-permute-start(f32[5,64,256]{2,1,0:T(8,128)S(1)} %get-tuple-element.577), channel_id=1, source_target_pairs={{0,16},{16,32},{32,48},{48,64},{64,80},{80,96},{96,112},{112,128},... | collective-permute-start | bytes 983048 | tf_op jit(solution)/shard_map/while/body/eval_jaxpr/ppermute | solution.py:14
  241.3 6.5 %collective-permute-start = (f32[5,64,256]{2,1,0:T(8,128)S(1)}, f32[5,64,256]{2,1,0:T(8,128)S(1)}, u32[]{:S(2)}, u32[]{:S(2)}) collective-permute-start(f32[5,64,256]{2,1,0:T(8,128)S(1)} %get-tuple-element.577), channel_id=1, source_target_pairs={{0,16},{16,32},{32,48},{48,64},{64,80},{80,96},{96,112},{112,128},... | collective-permute-start | bytes 983048 | tf_op jit(solution)/shard_map/while/body/eval_jaxpr/ppermute | solution.py:14
  258.3 199.1 %while.37 = (s32[]{:T(128)}, f32[5,4,64,256]{3,2,0,1:T(8,128)}, f32[5,64,256]{2,1,0:T(8,128)S(1)}, s32[]{:T(128)}, f32[5,4,64,256]{3,2,1,0:T(8,128)S(1)}, /*inde...) while((s32[]{:T(128)}, f32[5,4,64,256]{3,2,0,1:T(8,128)}, ...), condition=%wide.region_7.8_spmd, body=%wide.region_4.7_spmd.sunk | while | flops 4259847 | bytes 12715819 | solution.py:123
  260.3 10.3 %collective-permute-done.1 = f32[5,64,256]{2,1,0:T(8,128)S(1)} collective-permute-done((f32[5,64,256]{2,1,0:T(8,128)S(1)}, f32[5,64,256]{2,1,0:T(8,128)S(1)}, u32[]{:S(2)}, u32[]{:S(2)}) %collective-permute-start.1) | collective-permute-done | bytes 327712 | tf_op jit(solution)/shard_map/while/body/eval_jaxpr/ppermute | solution.py:14
  272.5 11.4 %collective-permute-done.1 = f32[5,64,256]{2,1,0:T(8,128)S(1)} collective-permute-done((f32[5,64,256]{2,1,0:T(8,128)S(1)}, f32[5,64,256]{2,1,0:T(8,128)S(1)}, u32[]{:S(2)}, u32[]{:S(2)}) %collective-permute-start.1) | collective-permute-done | bytes 327712 | tf_op jit(solution)/shard_map/while/body/eval_jaxpr/ppermute | solution.py:14
  285.9 10.2 %collective-permute-done.1 = f32[5,64,256]{2,1,0:T(8,128)S(1)} collective-permute-done((f32[5,64,256]{2,1,0:T(8,128)S(1)}, f32[5,64,256]{2,1,0:T(8,128)S(1)}, u32[]{:S(2)}, u32[]{:S(2)}) %collective-permute-start.1) | collective-permute-done | bytes 327712 | tf_op jit(solution)/shard_map/while/body/eval_jaxpr/ppermute | solution.py:14
  298.1 12.7 %collective-permute-done.1 = f32[5,64,256]{2,1,0:T(8,128)S(1)} collective-permute-done((f32[5,64,256]{2,1,0:T(8,128)S(1)}, f32[5,64,256]{2,1,0:T(8,128)S(1)}, u32[]{:S(2)}, u32[]{:S(2)}) %collective-permute-start.1) | collective-permute-done | bytes 327712 | tf_op jit(solution)/shard_map/while/body/eval_jaxpr/ppermute | solution.py:14
  314.7 10.1 %collective-permute-done.1 = f32[5,64,256]{2,1,0:T(8,128)S(1)} collective-permute-done((f32[5,64,256]{2,1,0:T(8,128)S(1)}, f32[5,64,256]{2,1,0:T(8,128)S(1)}, u32[]{:S(2)}, u32[]{:S(2)}) %collective-permute-start.1) | collective-permute-done | bytes 327712 | tf_op jit(solution)/shard_map/while/body/eval_jaxpr/ppermute | solution.py:14
  327.0 9.0 %collective-permute-done.1 = f32[5,64,256]{2,1,0:T(8,128)S(1)} collective-permute-done((f32[5,64,256]{2,1,0:T(8,128)S(1)}, f32[5,64,256]{2,1,0:T(8,128)S(1)}, u32[]{:S(2)}, u32[]{:S(2)}) %collective-permute-start.1) | collective-permute-done | bytes 327712 | tf_op jit(solution)/shard_map/while/body/eval_jaxpr/ppermute | solution.py:14
  338.0 9.1 %collective-permute-done.1 = f32[5,64,256]{2,1,0:T(8,128)S(1)} collective-permute-done((f32[5,64,256]{2,1,0:T(8,128)S(1)}, f32[5,64,256]{2,1,0:T(8,128)S(1)}, u32[]{:S(2)}, u32[]{:S(2)}) %collective-permute-start.1) | collective-permute-done | bytes 327712 | tf_op jit(solution)/shard_map/while/body/eval_jaxpr/ppermute | solution.py:14
  349.1 9.1 %collective-permute-done.1 = f32[5,64,256]{2,1,0:T(8,128)S(1)} collective-permute-done((f32[5,64,256]{2,1,0:T(8,128)S(1)}, f32[5,64,256]{2,1,0:T(8,128)S(1)}, u32[]{:S(2)}, u32[]{:S(2)}) %collective-permute-start.1) | collective-permute-done | bytes 327712 | tf_op jit(solution)/shard_map/while/body/eval_jaxpr/ppermute | solution.py:14
  360.2 9.6 %collective-permute-done.1 = f32[5,64,256]{2,1,0:T(8,128)S(1)} collective-permute-done((f32[5,64,256]{2,1,0:T(8,128)S(1)}, f32[5,64,256]{2,1,0:T(8,128)S(1)}, u32[]{:S(2)}, u32[]{:S(2)}) %collective-permute-start.1) | collective-permute-done | bytes 327712 | tf_op jit(solution)/shard_map/while/body/eval_jaxpr/ppermute | solution.py:14
  371.8 10.7 %collective-permute-done.1 = f32[5,64,256]{2,1,0:T(8,128)S(1)} collective-permute-done((f32[5,64,256]{2,1,0:T(8,128)S(1)}, f32[5,64,256]{2,1,0:T(8,128)S(1)}, u32[]{:S(2)}, u32[]{:S(2)}) %collective-permute-start.1) | collective-permute-done | bytes 327712 | tf_op jit(solution)/shard_map/while/body/eval_jaxpr/ppermute | solution.py:14
  384.4 11.8 %collective-permute-done.1 = f32[5,64,256]{2,1,0:T(8,128)S(1)} collective-permute-done((f32[5,64,256]{2,1,0:T(8,128)S(1)}, f32[5,64,256]{2,1,0:T(8,128)S(1)}, u32[]{:S(2)}, u32[]{:S(2)}) %collective-permute-start.1) | collective-permute-done | bytes 327712 | tf_op jit(solution)/shard_map/while/body/eval_jaxpr/ppermute | solution.py:14
  398.2 12.3 %collective-permute-done.1 = f32[5,64,256]{2,1,0:T(8,128)S(1)} collective-permute-done((f32[5,64,256]{2,1,0:T(8,128)S(1)}, f32[5,64,256]{2,1,0:T(8,128)S(1)}, u32[]{:S(2)}, u32[]{:S(2)}) %collective-permute-start.1) | collective-permute-done | bytes 327712 | tf_op jit(solution)/shard_map/while/body/eval_jaxpr/ppermute | solution.py:14
  412.5 11.5 %collective-permute-done.1 = f32[5,64,256]{2,1,0:T(8,128)S(1)} collective-permute-done((f32[5,64,256]{2,1,0:T(8,128)S(1)}, f32[5,64,256]{2,1,0:T(8,128)S(1)}, u32[]{:S(2)}, u32[]{:S(2)}) %collective-permute-start.1) | collective-permute-done | bytes 327712 | tf_op jit(solution)/shard_map/while/body/eval_jaxpr/ppermute | solution.py:14
  425.9 9.1 %collective-permute-done.1 = f32[5,64,256]{2,1,0:T(8,128)S(1)} collective-permute-done((f32[5,64,256]{2,1,0:T(8,128)S(1)}, f32[5,64,256]{2,1,0:T(8,128)S(1)}, u32[]{:S(2)}, u32[]{:S(2)}) %collective-permute-start.1) | collective-permute-done | bytes 327712 | tf_op jit(solution)/shard_map/while/body/eval_jaxpr/ppermute | solution.py:14
  437.1 9.1 %collective-permute-done.1 = f32[5,64,256]{2,1,0:T(8,128)S(1)} collective-permute-done((f32[5,64,256]{2,1,0:T(8,128)S(1)}, f32[5,64,256]{2,1,0:T(8,128)S(1)}, u32[]{:S(2)}, u32[]{:S(2)}) %collective-permute-start.1) | collective-permute-done | bytes 327712 | tf_op jit(solution)/shard_map/while/body/eval_jaxpr/ppermute | solution.py:14
  448.2 9.1 %collective-permute-done.1 = f32[5,64,256]{2,1,0:T(8,128)S(1)} collective-permute-done((f32[5,64,256]{2,1,0:T(8,128)S(1)}, f32[5,64,256]{2,1,0:T(8,128)S(1)}, u32[]{:S(2)}, u32[]{:S(2)}) %collective-permute-start.1) | collective-permute-done | bytes 327712 | tf_op jit(solution)/shard_map/while/body/eval_jaxpr/ppermute | solution.py:14
  (187 shorter events, 110.7 us)
Async XLA Ops:
  4.6 4.7 %collective-permute-start.3 = (f32[10,4,1,256]{3,1,2,0:T(4,128)}, f32[10,4,1,256]{3,1,2,0:T(4,128)S(1)}, u32[]{:S(2)}, u32[]{:S(2)}) collective-permute-start(f32[10,4,1,256]{3,1,2,0:T(4,128)} %get-tuple-element.477), channel_id=1, source_target_pairs={{8,0},{9,1},{10,2},{11,3},{12,4},{13,5},{14,6},{15,7},{24,16},{25,... | collective-permute-start | bytes 122888 | tf_op jit(solution)/shard_map/ppermute | solution.py:27
  5.9 3.9 collective-permute-start.2
  10.4 2.5 copy-start.2
  16.2 15.6 %collective-permute-start.5 = (f32[10,4,66,1]{2,1,3,0:T(4,128)S(1)}, f32[10,4,66,1]{2,1,3,0:T(4,128)S(1)}, u32[]{:S(2)}, u32[]{:S(2)}) collective-permute-start(f32[10,4,66,1]{2,1,3,0:T(4,128)S(1)} %copy.40), channel_id=1, source_target_pairs={{1,0},{2,1},{3,2},{4,3},{5,4},{6,5},{7,6},{9,8},{10,9},{11,10},{12... | collective-permute-start | bytes 31688 | tf_op jit(solution)/shard_map/ppermute | solution.py:27
  20.1 13.4 %collective-permute-start.4 = (f32[10,4,66,1]{2,1,3,0:T(4,128)S(1)}, f32[10,4,66,1]{2,1,3,0:T(4,128)}, u32[]{:S(2)}, u32[]{:S(2)}) collective-permute-start(f32[10,4,66,1]{2,1,3,0:T(4,128)S(1)} %copy.39), channel_id=1, source_target_pairs={{0,1},{1,2},{2,3},{3,4},{4,5},{5,6},{6,7},{8,9},{9,10},{10,11},{11... | collective-permute-start | bytes 31688 | tf_op jit(solution)/shard_map/ppermute | solution.py:25
  25.1 3.9 copy-start.3
  29.0 2.1 copy-start.13
  35.9 1.9 copy-start.1
  45.5 5.0 %copy-start.7 = (f32[5,4,64,258]{3,1,2,0:T(4,128)}, f32[5,4,64,258]{3,1,2,0:T(4,128)S(1)}, u32[]{:S(2)}) copy-start(f32[5,4,64,258]{3,1,2,0:T(4,128)S(1)} %slice.432) | copy-start | bytes 3962884
  50.3 1.8 copy-start.5
  50.4 2.4 copy-start.6
  50.4 2.8 copy-start.10
  50.4 2.8 copy-start.15
  50.6 4.5 copy-start.8
  56.7 195.7 %copy-start.12 = (f32[4,64,256]{2,0,1:T(4,128)S(1)}, f32[4,64,256]{2,0,1:T(4,128)}, u32[]{:S(2)}) copy-start(f32[4,64,256]{2,0,1:T(4,128)} %copy-done.11) | copy-start | bytes 786436
  56.7 195.7 %copy-start.14 = (f32[4,64,256]{2,0,1:T(4,128)S(1)}, f32[4,64,256]{2,0,1:T(4,128)}, u32[]{:S(2)}) copy-start(f32[4,64,256]{2,0,1:T(4,128)} %slice.436) | copy-start | bytes 786436
  56.8 11.6 %collective-permute-start = (f32[5,64,256]{2,1,0:T(8,128)S(1)}, f32[5,64,256]{2,1,0:T(8,128)S(1)}, u32[]{:S(2)}, u32[]{:S(2)}) collective-permute-start(f32[5,64,256]{2,1,0:T(8,128)S(1)} %get-tuple-element.577), channel_id=1, source_target_pairs={{0,16},{16,32},{32,48},{48,64},{64,80},{80,96},{96,112},{112,128},... | collective-permute-start | bytes 983048 | tf_op jit(solution)/shard_map/while/body/eval_jaxpr/ppermute | solution.py:14
  68.5 11.5 %collective-permute-start = (f32[5,64,256]{2,1,0:T(8,128)S(1)}, f32[5,64,256]{2,1,0:T(8,128)S(1)}, u32[]{:S(2)}, u32[]{:S(2)}) collective-permute-start(f32[5,64,256]{2,1,0:T(8,128)S(1)} %get-tuple-element.577), channel_id=1, source_target_pairs={{0,16},{16,32},{32,48},{48,64},{64,80},{80,96},{96,112},{112,128},... | collective-permute-start | bytes 983048 | tf_op jit(solution)/shard_map/while/body/eval_jaxpr/ppermute | solution.py:14
  80.0 11.8 %collective-permute-start = (f32[5,64,256]{2,1,0:T(8,128)S(1)}, f32[5,64,256]{2,1,0:T(8,128)S(1)}, u32[]{:S(2)}, u32[]{:S(2)}) collective-permute-start(f32[5,64,256]{2,1,0:T(8,128)S(1)} %get-tuple-element.577), channel_id=1, source_target_pairs={{0,16},{16,32},{32,48},{48,64},{64,80},{80,96},{96,112},{112,128},... | collective-permute-start | bytes 983048 | tf_op jit(solution)/shard_map/while/body/eval_jaxpr/ppermute | solution.py:14
  91.8 11.1 %collective-permute-start = (f32[5,64,256]{2,1,0:T(8,128)S(1)}, f32[5,64,256]{2,1,0:T(8,128)S(1)}, u32[]{:S(2)}, u32[]{:S(2)}) collective-permute-start(f32[5,64,256]{2,1,0:T(8,128)S(1)} %get-tuple-element.577), channel_id=1, source_target_pairs={{0,16},{16,32},{32,48},{48,64},{64,80},{80,96},{96,112},{112,128},... | collective-permute-start | bytes 983048 | tf_op jit(solution)/shard_map/while/body/eval_jaxpr/ppermute | solution.py:14
  103.0 11.1 %collective-permute-start = (f32[5,64,256]{2,1,0:T(8,128)S(1)}, f32[5,64,256]{2,1,0:T(8,128)S(1)}, u32[]{:S(2)}, u32[]{:S(2)}) collective-permute-start(f32[5,64,256]{2,1,0:T(8,128)S(1)} %get-tuple-element.577), channel_id=1, source_target_pairs={{0,16},{16,32},{32,48},{48,64},{64,80},{80,96},{96,112},{112,128},... | collective-permute-start | bytes 983048 | tf_op jit(solution)/shard_map/while/body/eval_jaxpr/ppermute | solution.py:14
  114.1 11.1 %collective-permute-start = (f32[5,64,256]{2,1,0:T(8,128)S(1)}, f32[5,64,256]{2,1,0:T(8,128)S(1)}, u32[]{:S(2)}, u32[]{:S(2)}) collective-permute-start(f32[5,64,256]{2,1,0:T(8,128)S(1)} %get-tuple-element.577), channel_id=1, source_target_pairs={{0,16},{16,32},{32,48},{48,64},{64,80},{80,96},{96,112},{112,128},... | collective-permute-start | bytes 983048 | tf_op jit(solution)/shard_map/while/body/eval_jaxpr/ppermute | solution.py:14
  125.2 11.7 %collective-permute-start = (f32[5,64,256]{2,1,0:T(8,128)S(1)}, f32[5,64,256]{2,1,0:T(8,128)S(1)}, u32[]{:S(2)}, u32[]{:S(2)}) collective-permute-start(f32[5,64,256]{2,1,0:T(8,128)S(1)} %get-tuple-element.577), channel_id=1, source_target_pairs={{0,16},{16,32},{32,48},{48,64},{64,80},{80,96},{96,112},{112,128},... | collective-permute-start | bytes 983048 | tf_op jit(solution)/shard_map/while/body/eval_jaxpr/ppermute | solution.py:14
  136.9 12.8 %collective-permute-start = (f32[5,64,256]{2,1,0:T(8,128)S(1)}, f32[5,64,256]{2,1,0:T(8,128)S(1)}, u32[]{:S(2)}, u32[]{:S(2)}) collective-permute-start(f32[5,64,256]{2,1,0:T(8,128)S(1)} %get-tuple-element.577), channel_id=1, source_target_pairs={{0,16},{16,32},{32,48},{48,64},{64,80},{80,96},{96,112},{112,128},... | collective-permute-start | bytes 983048 | tf_op jit(solution)/shard_map/while/body/eval_jaxpr/ppermute | solution.py:14
  149.8 14.0 %collective-permute-start = (f32[5,64,256]{2,1,0:T(8,128)S(1)}, f32[5,64,256]{2,1,0:T(8,128)S(1)}, u32[]{:S(2)}, u32[]{:S(2)}) collective-permute-start(f32[5,64,256]{2,1,0:T(8,128)S(1)} %get-tuple-element.577), channel_id=1, source_target_pairs={{0,16},{16,32},{32,48},{48,64},{64,80},{80,96},{96,112},{112,128},... | collective-permute-start | bytes 983048 | tf_op jit(solution)/shard_map/while/body/eval_jaxpr/ppermute | solution.py:14
  163.8 14.1 %collective-permute-start = (f32[5,64,256]{2,1,0:T(8,128)S(1)}, f32[5,64,256]{2,1,0:T(8,128)S(1)}, u32[]{:S(2)}, u32[]{:S(2)}) collective-permute-start(f32[5,64,256]{2,1,0:T(8,128)S(1)} %get-tuple-element.577), channel_id=1, source_target_pairs={{0,16},{16,32},{32,48},{48,64},{64,80},{80,96},{96,112},{112,128},... | collective-permute-start | bytes 983048 | tf_op jit(solution)/shard_map/while/body/eval_jaxpr/ppermute | solution.py:14
  177.9 13.3 %collective-permute-start = (f32[5,64,256]{2,1,0:T(8,128)S(1)}, f32[5,64,256]{2,1,0:T(8,128)S(1)}, u32[]{:S(2)}, u32[]{:S(2)}) collective-permute-start(f32[5,64,256]{2,1,0:T(8,128)S(1)} %get-tuple-element.577), channel_id=1, source_target_pairs={{0,16},{16,32},{32,48},{48,64},{64,80},{80,96},{96,112},{112,128},... | collective-permute-start | bytes 983048 | tf_op jit(solution)/shard_map/while/body/eval_jaxpr/ppermute | solution.py:14
  193.2 12.4 %collective-permute-start = (f32[5,64,256]{2,1,0:T(8,128)S(1)}, f32[5,64,256]{2,1,0:T(8,128)S(1)}, u32[]{:S(2)}, u32[]{:S(2)}) collective-permute-start(f32[5,64,256]{2,1,0:T(8,128)S(1)} %get-tuple-element.577), channel_id=1, source_target_pairs={{0,16},{16,32},{32,48},{48,64},{64,80},{80,96},{96,112},{112,128},... | collective-permute-start | bytes 983048 | tf_op jit(solution)/shard_map/while/body/eval_jaxpr/ppermute | solution.py:14
  205.6 13.5 %collective-permute-start = (f32[5,64,256]{2,1,0:T(8,128)S(1)}, f32[5,64,256]{2,1,0:T(8,128)S(1)}, u32[]{:S(2)}, u32[]{:S(2)}) collective-permute-start(f32[5,64,256]{2,1,0:T(8,128)S(1)} %get-tuple-element.577), channel_id=1, source_target_pairs={{0,16},{16,32},{32,48},{48,64},{64,80},{80,96},{96,112},{112,128},... | collective-permute-start | bytes 983048 | tf_op jit(solution)/shard_map/while/body/eval_jaxpr/ppermute | solution.py:14
  219.1 11.1 %collective-permute-start = (f32[5,64,256]{2,1,0:T(8,128)S(1)}, f32[5,64,256]{2,1,0:T(8,128)S(1)}, u32[]{:S(2)}, u32[]{:S(2)}) collective-permute-start(f32[5,64,256]{2,1,0:T(8,128)S(1)} %get-tuple-element.577), channel_id=1, source_target_pairs={{0,16},{16,32},{32,48},{48,64},{64,80},{80,96},{96,112},{112,128},... | collective-permute-start | bytes 983048 | tf_op jit(solution)/shard_map/while/body/eval_jaxpr/ppermute | solution.py:14
  230.2 11.1 %collective-permute-start = (f32[5,64,256]{2,1,0:T(8,128)S(1)}, f32[5,64,256]{2,1,0:T(8,128)S(1)}, u32[]{:S(2)}, u32[]{:S(2)}) collective-permute-start(f32[5,64,256]{2,1,0:T(8,128)S(1)} %get-tuple-element.577), channel_id=1, source_target_pairs={{0,16},{16,32},{32,48},{48,64},{64,80},{80,96},{96,112},{112,128},... | collective-permute-start | bytes 983048 | tf_op jit(solution)/shard_map/while/body/eval_jaxpr/ppermute | solution.py:14
  241.3 11.1 %collective-permute-start = (f32[5,64,256]{2,1,0:T(8,128)S(1)}, f32[5,64,256]{2,1,0:T(8,128)S(1)}, u32[]{:S(2)}, u32[]{:S(2)}) collective-permute-start(f32[5,64,256]{2,1,0:T(8,128)S(1)} %get-tuple-element.577), channel_id=1, source_target_pairs={{0,16},{16,32},{32,48},{48,64},{64,80},{80,96},{96,112},{112,128},... | collective-permute-start | bytes 983048 | tf_op jit(solution)/shard_map/while/body/eval_jaxpr/ppermute | solution.py:14
  258.3 12.2 %collective-permute-start.1 = (f32[5,64,256]{2,1,0:T(8,128)S(1)}, f32[5,64,256]{2,1,0:T(8,128)S(1)}, u32[]{:S(2)}, u32[]{:S(2)}) collective-permute-start(f32[5,64,256]{2,1,0:T(8,128)S(1)} %get-tuple-element.587), channel_id=1, source_target_pairs={{16,0},{32,16},{48,32},{64,48},{80,64},{96,80},{112,96},{128,112},... | collective-permute-start | bytes 983048 | tf_op jit(solution)/shard_map/while/body/eval_jaxpr/ppermute | solution.py:14
  270.6 13.3 %collective-permute-start.1 = (f32[5,64,256]{2,1,0:T(8,128)S(1)}, f32[5,64,256]{2,1,0:T(8,128)S(1)}, u32[]{:S(2)}, u32[]{:S(2)}) collective-permute-start(f32[5,64,256]{2,1,0:T(8,128)S(1)} %get-tuple-element.587), channel_id=1, source_target_pairs={{16,0},{32,16},{48,32},{64,48},{80,64},{96,80},{112,96},{128,112},... | collective-permute-start | bytes 983048 | tf_op jit(solution)/shard_map/while/body/eval_jaxpr/ppermute | solution.py:14
  284.0 12.1 %collective-permute-start.1 = (f32[5,64,256]{2,1,0:T(8,128)S(1)}, f32[5,64,256]{2,1,0:T(8,128)S(1)}, u32[]{:S(2)}, u32[]{:S(2)}) collective-permute-start(f32[5,64,256]{2,1,0:T(8,128)S(1)} %get-tuple-element.587), channel_id=1, source_target_pairs={{16,0},{32,16},{48,32},{64,48},{80,64},{96,80},{112,96},{128,112},... | collective-permute-start | bytes 983048 | tf_op jit(solution)/shard_map/while/body/eval_jaxpr/ppermute | solution.py:14
  296.1 14.6 %collective-permute-start.1 = (f32[5,64,256]{2,1,0:T(8,128)S(1)}, f32[5,64,256]{2,1,0:T(8,128)S(1)}, u32[]{:S(2)}, u32[]{:S(2)}) collective-permute-start(f32[5,64,256]{2,1,0:T(8,128)S(1)} %get-tuple-element.587), channel_id=1, source_target_pairs={{16,0},{32,16},{48,32},{64,48},{80,64},{96,80},{112,96},{128,112},... | collective-permute-start | bytes 983048 | tf_op jit(solution)/shard_map/while/body/eval_jaxpr/ppermute | solution.py:14
  312.8 12.0 %collective-permute-start.1 = (f32[5,64,256]{2,1,0:T(8,128)S(1)}, f32[5,64,256]{2,1,0:T(8,128)S(1)}, u32[]{:S(2)}, u32[]{:S(2)}) collective-permute-start(f32[5,64,256]{2,1,0:T(8,128)S(1)} %get-tuple-element.587), channel_id=1, source_target_pairs={{16,0},{32,16},{48,32},{64,48},{80,64},{96,80},{112,96},{128,112},... | collective-permute-start | bytes 983048 | tf_op jit(solution)/shard_map/while/body/eval_jaxpr/ppermute | solution.py:14
  324.9 11.1 %collective-permute-start.1 = (f32[5,64,256]{2,1,0:T(8,128)S(1)}, f32[5,64,256]{2,1,0:T(8,128)S(1)}, u32[]{:S(2)}, u32[]{:S(2)}) collective-permute-start(f32[5,64,256]{2,1,0:T(8,128)S(1)} %get-tuple-element.587), channel_id=1, source_target_pairs={{16,0},{32,16},{48,32},{64,48},{80,64},{96,80},{112,96},{128,112},... | collective-permute-start | bytes 983048 | tf_op jit(solution)/shard_map/while/body/eval_jaxpr/ppermute | solution.py:14
  336.0 11.1 %collective-permute-start.1 = (f32[5,64,256]{2,1,0:T(8,128)S(1)}, f32[5,64,256]{2,1,0:T(8,128)S(1)}, u32[]{:S(2)}, u32[]{:S(2)}) collective-permute-start(f32[5,64,256]{2,1,0:T(8,128)S(1)} %get-tuple-element.587), channel_id=1, source_target_pairs={{16,0},{32,16},{48,32},{64,48},{80,64},{96,80},{112,96},{128,112},... | collective-permute-start | bytes 983048 | tf_op jit(solution)/shard_map/while/body/eval_jaxpr/ppermute | solution.py:14
  347.1 11.1 %collective-permute-start.1 = (f32[5,64,256]{2,1,0:T(8,128)S(1)}, f32[5,64,256]{2,1,0:T(8,128)S(1)}, u32[]{:S(2)}, u32[]{:S(2)}) collective-permute-start(f32[5,64,256]{2,1,0:T(8,128)S(1)} %get-tuple-element.587), channel_id=1, source_target_pairs={{16,0},{32,16},{48,32},{64,48},{80,64},{96,80},{112,96},{128,112},... | collective-permute-start | bytes 983048 | tf_op jit(solution)/shard_map/while/body/eval_jaxpr/ppermute | solution.py:14
  358.3 11.5 %collective-permute-start.1 = (f32[5,64,256]{2,1,0:T(8,128)S(1)}, f32[5,64,256]{2,1,0:T(8,128)S(1)}, u32[]{:S(2)}, u32[]{:S(2)}) collective-permute-start(f32[5,64,256]{2,1,0:T(8,128)S(1)} %get-tuple-element.587), channel_id=1, source_target_pairs={{16,0},{32,16},{48,32},{64,48},{80,64},{96,80},{112,96},{128,112},... | collective-permute-start | bytes 983048 | tf_op jit(solution)/shard_map/while/body/eval_jaxpr/ppermute | solution.py:14
  369.8 12.6 %collective-permute-start.1 = (f32[5,64,256]{2,1,0:T(8,128)S(1)}, f32[5,64,256]{2,1,0:T(8,128)S(1)}, u32[]{:S(2)}, u32[]{:S(2)}) collective-permute-start(f32[5,64,256]{2,1,0:T(8,128)S(1)} %get-tuple-element.587), channel_id=1, source_target_pairs={{16,0},{32,16},{48,32},{64,48},{80,64},{96,80},{112,96},{128,112},... | collective-permute-start | bytes 983048 | tf_op jit(solution)/shard_map/while/body/eval_jaxpr/ppermute | solution.py:14
  382.5 13.8 %collective-permute-start.1 = (f32[5,64,256]{2,1,0:T(8,128)S(1)}, f32[5,64,256]{2,1,0:T(8,128)S(1)}, u32[]{:S(2)}, u32[]{:S(2)}) collective-permute-start(f32[5,64,256]{2,1,0:T(8,128)S(1)} %get-tuple-element.587), channel_id=1, source_target_pairs={{16,0},{32,16},{48,32},{64,48},{80,64},{96,80},{112,96},{128,112},... | collective-permute-start | bytes 983048 | tf_op jit(solution)/shard_map/while/body/eval_jaxpr/ppermute | solution.py:14
  396.3 14.3 %collective-permute-start.1 = (f32[5,64,256]{2,1,0:T(8,128)S(1)}, f32[5,64,256]{2,1,0:T(8,128)S(1)}, u32[]{:S(2)}, u32[]{:S(2)}) collective-permute-start(f32[5,64,256]{2,1,0:T(8,128)S(1)} %get-tuple-element.587), channel_id=1, source_target_pairs={{16,0},{32,16},{48,32},{64,48},{80,64},{96,80},{112,96},{128,112},... | collective-permute-start | bytes 983048 | tf_op jit(solution)/shard_map/while/body/eval_jaxpr/ppermute | solution.py:14
  410.6 13.4 %collective-permute-start.1 = (f32[5,64,256]{2,1,0:T(8,128)S(1)}, f32[5,64,256]{2,1,0:T(8,128)S(1)}, u32[]{:S(2)}, u32[]{:S(2)}) collective-permute-start(f32[5,64,256]{2,1,0:T(8,128)S(1)} %get-tuple-element.587), channel_id=1, source_target_pairs={{16,0},{32,16},{48,32},{64,48},{80,64},{96,80},{112,96},{128,112},... | collective-permute-start | bytes 983048 | tf_op jit(solution)/shard_map/while/body/eval_jaxpr/ppermute | solution.py:14
  424.0 11.1 %collective-permute-start.1 = (f32[5,64,256]{2,1,0:T(8,128)S(1)}, f32[5,64,256]{2,1,0:T(8,128)S(1)}, u32[]{:S(2)}, u32[]{:S(2)}) collective-permute-start(f32[5,64,256]{2,1,0:T(8,128)S(1)} %get-tuple-element.587), channel_id=1, source_target_pairs={{16,0},{32,16},{48,32},{64,48},{80,64},{96,80},{112,96},{128,112},... | collective-permute-start | bytes 983048 | tf_op jit(solution)/shard_map/while/body/eval_jaxpr/ppermute | solution.py:14
  435.1 11.1 %collective-permute-start.1 = (f32[5,64,256]{2,1,0:T(8,128)S(1)}, f32[5,64,256]{2,1,0:T(8,128)S(1)}, u32[]{:S(2)}, u32[]{:S(2)}) collective-permute-start(f32[5,64,256]{2,1,0:T(8,128)S(1)} %get-tuple-element.587), channel_id=1, source_target_pairs={{16,0},{32,16},{48,32},{64,48},{80,64},{96,80},{112,96},{128,112},... | collective-permute-start | bytes 983048 | tf_op jit(solution)/shard_map/while/body/eval_jaxpr/ppermute | solution.py:14
  446.3 11.1 %collective-permute-start.1 = (f32[5,64,256]{2,1,0:T(8,128)S(1)}, f32[5,64,256]{2,1,0:T(8,128)S(1)}, u32[]{:S(2)}, u32[]{:S(2)}) collective-permute-start(f32[5,64,256]{2,1,0:T(8,128)S(1)} %get-tuple-element.587), channel_id=1, source_target_pairs={{16,0},{32,16},{48,32},{64,48},{80,64},{96,80},{112,96},{128,112},... | collective-permute-start | bytes 983048 | tf_op jit(solution)/shard_map/while/body/eval_jaxpr/ppermute | solution.py:14
  (4 other events, 5.5 us)
where the time goes:
time: 461 us; the launch traced here: 460 us
  waiting for transfers between devices  259 us (56%)
  starting transfers between devices  142 us (31%)
  other arithmetic  33 us (7%)
  local copies, waits for them, and re-layouts  24.5 us (5%)
    ppermute x32, waiting for transfers between devices, shifted(): lax.ppermute(value, axis, [(source, source + steps) for source in range(i...  259 us
    ppermute x32, starting transfers between devices, shifted(): lax.ppermute(value, axis, [(source, source + steps) for source in range(i...  130 us
  transfers between devices with their start and end apart: 36, of which 33 were waited for; matrix products, arithmetic and copies ran while one was open for 2% of the time, Pallas kernels for 0%

commit v1 on v0

v1 whole, which is shorter than its diff:
```python
import functools
import math

import jax
import jax.numpy as jnp
from jax import lax
from jax.experimental import pallas as pl
from jax.experimental.pallas import tpu as pltpu
from jax.sharding import PartitionSpec as P

MESH = pl.DeviceIdType.MESH
ROOT2 = math.sqrt(2.0)
ADIABATIC = 1.4
COUPLING = 0.7
METRIC = (0.1, 0.1, 1.0)
CLASS = (0, 1, 2, 2, 2)
DEPTH = 4
NCOEF = 9
NTERM = 10


def tile_of(value, half):
    return value[:, 128 * half : 128 * (half + 1)]


def sweep_kernel(
    sections, gy_count, blocks,
    cons_hbm, res_hbm, out_hbm,
    cons, res, gain, base_part, up_part, faces, pull, part, scale,
    coef_out, coef_in, term_out, term_in, link_out, link_in,
    ys, yr, result,
    load_sem, coef_ssem, coef_rsem, term_ssem, term_rsem, link_ssem, link_rsem,
    halo_ssem, halo_rsem, store_sem,
):
    me = lax.axis_index("gz")
    gx = lax.axis_index("gx")
    gy = lax.axis_index("gy")
    above = lax.rem(gy + 1, gy_count)
    below = lax.rem(gy + gy_count - 1, gy_count)

    def first_block(step):
        return lax.rem(me // 2 + step, blocks)

    def loads(step):
        rows = pl.ds(pl.multiple_of(8 * first_block(step), 8), 8)
        return (
            pltpu.make_async_copy(cons_hbm.at[:, :, rows, :], cons.at[:, :, rows, :], load_sem.at[0, step]),
            pltpu.make_async_copy(res_hbm.at[:, :, rows, :], res.at[:, :, rows, :], load_sem.at[1, step]),
        )

    def start_load(step, carry):
        for copy in loads(step):
            copy.start()
        return carry

    lax.fori_loop(0, blocks, start_load, 0)

    barrier = pltpu.get_barrier_semaphore()

    def greet(step, carry):
        pl.semaphore_signal(
            barrier, inc=1, device_id={"gz": lax.rem(me + step, sections)}, device_id_type=MESH
        )
        return carry

    lax.fori_loop(1, sections, greet, 0)
    pl.semaphore_signal(barrier, inc=1, device_id={"gx": 1 - gx}, device_id_type=MESH)
    pl.semaphore_signal(barrier, inc=1, device_id={"gy": above}, device_id_type=MESH)
    pl.semaphore_signal(barrier, inc=1, device_id={"gy": below}, device_id_type=MESH)

    lane = lax.broadcasted_iota(jnp.int32, (8, 256), 1)
    sublane = lax.broadcasted_iota(jnp.int32, (8, 256), 0)
    small_lane = lax.broadcasted_iota(jnp.int32, (8, 128), 1)

    def coef_copy(tile, slot):
        return pltpu.make_async_remote_copy(
            src_ref=coef_out.at[tile], dst_ref=coef_in.at[slot],
            send_sem=coef_ssem.at[tile], recv_sem=coef_rsem.at[slot],
            device_id={"gz": tile}, device_id_type=MESH,
        )

    def term_copy(tile, slot):
        return pltpu.make_async_remote_copy(
            src_ref=term_out.at[tile], dst_ref=term_in.at[slot],
            send_sem=term_ssem.at[tile], recv_sem=term_rsem.at[slot],
            device_id={"gz": tile}, device_id_type=MESH,
        )

    def link_copy(section, slot):
        return pltpu.make_async_remote_copy(
            src_ref=link_out.at[section], dst_ref=link_in.at[slot],
            send_sem=link_ssem.at[section], recv_sem=link_rsem.at[slot],
            device_id={"gz": section}, device_id_type=MESH,
        )

    def first_pass(step, carry):
        block = first_block(step)
        for copy in loads(step):
            copy.wait()
        rows = pl.ds(pl.multiple_of(8 * block, 8), 8)
        edge_low = jnp.zeros((8, 128), jnp.float32)
        edge_high = jnp.zeros((8, 128), jnp.float32)
        alphas, betas = [], []
        for k in range(DEPTH):
            density = cons[0, k, rows, :]
            inverse = 1.0 / density
            velocity = [cons[1 + d, k, rows, :] * inverse for d in range(3)]
            kinetic = 0.5 * density * (
                velocity[0] * velocity[0] + velocity[1] * velocity[1] + velocity[2] * velocity[2]
            )
            pressure = (ADIABATIC - 1.0) * (cons[4, k, rows, :] - kinetic)
            sound = jnp.sqrt(ADIABATIC * pressure * inverse)
            radius = [jnp.abs(velocity[d]) + sound for d in range(3)]
            diagonal = METRIC[0] * radius[0] + METRIC[1] * radius[1] + METRIC[2] * radius[2]
            rdiag = 1.0 / diagonal
            half = (0.5 * METRIC[2]) * rdiag
            forward = (velocity[2] + radius[2]) * half
            backward = (radius[2] - velocity[2]) * half
            skew = (0.5 * METRIC[2] * COUPLING * ROOT2) * sound * rdiag
            for h in range(2):
                gain[2 * block + h, k] = tile_of(forward, h)
                gain[2 * block + h, 4 + k] = tile_of(backward, h)
                gain[2 * block + h, 8 + k] = tile_of(skew, h)
                scale[2 * block + h, k] = tile_of(rdiag, h)
            alphas.append((forward + skew, forward - skew, forward))
            betas.append((backward - skew, backward + skew, backward))

            r = [res[f, k, rows, :] for f in range(5)]
            total = r[0] + r[4]
            third = ROOT2 * r[3]
            source = [-(total + third), third - total, r[4] - r[0], -r[1], -r[2]]
            guess = [value * rdiag for value in source]
            pair = -total * rdiag
            cross = {}
            for d in range(2):
                weight = 0.5 * METRIC[d]
                plus = weight * (velocity[d] + radius[d])
                minus = weight * (velocity[d] - radius[d])
                mix = (weight * COUPLING) * sound
                outer = 2.0 * mix * guess[3 + d]
                inner = mix * pair
                extra = [outer, outer, None, None, None]
                extra[3 + d] = inner
                cross[d] = (
                    [plus * v if x is None else plus * v + x for v, x in zip(guess, extra)],
                    [minus * v if x is None else minus * v + x for v, x in zip(guess, extra)],
                )
            for e in range(5):
                n = 4 * e + k
                xp = pltpu.roll(cross[0][0][e], 1, 0)
                xm = pltpu.roll(cross[0][1][e], 7, 0)
                faces[0, block + 1, n : n + 1, :] = xp[0:1]
                faces[1, block, n : n + 1, :] = xm[7:8]
                yp, ym = cross[1][0][e], cross[1][1][e]
                base_part[n, rows, :] = (
                    source[e]
                    + jnp.where(sublane == 0, 0.0, xp)
                    + jnp.where(lane == 0, 0.0, pltpu.roll(yp, 1, 1))
                )
                up_part[n, rows, :] = (
                    jnp.where(sublane == 7, 0.0, xm)
                    + jnp.where(lane == 255, 0.0, pltpu.roll(ym, 255, 1))
                )
                edge_high = jnp.where(
                    small_lane == n, pltpu.roll(tile_of(yp, 1), (n + 1) % 128, 1), edge_high
                )
                edge_low = jnp.where(small_lane == n, pltpu.roll(tile_of(ym, 0), n, 1), edge_low)
        ys[0, rows, :] = edge_high
        ys[1, rows, :] = edge_low

        coefs = [None] * NCOEF
        for c in range(3):
            a = [alphas[k][c] for k in range(DEPTH)]
            b = [betas[k][c] for k in range(DEPTH)]
            lead = [None, a[0], a[0] * a[1], a[0] * a[1] * a[2]]
            trail = [None] * DEPTH
            trail[2] = b[3]
            trail[1] = b[3] * b[2]
            trail[0] = trail[1] * b[1]
            reply = [None] * DEPTH
            reply[3] = lead[3]
            reply[2] = lead[2] + b[3] * reply[3]
            reply[1] = lead[1] + b[2] * reply[2]
            reply[0] = 1.0 + b[1] * reply[1]
            coefs[c] = lead[3] * a[3]
            coefs[3 + c] = trail[0] * b[0]
            coefs[6 + c] = reply[0] * b[0]
            for h in range(2):
                for k in range(DEPTH):
                    pull[2 * block + h, 4 * c + k] = tile_of(reply[k], h)
                    if k < 3:
                        pull[2 * block + h, 12 + 3 * c + k] = tile_of(trail[k], h)
        for h in range(2):
            for j in range(NCOEF):
                coef_out[2 * block + h, j] = tile_of(coefs[j], h)

        return carry

    def first_send(step, carry):
        block = first_block(step)
        for h in range(2):
            tile = 2 * block + h

            @pl.when(tile != me)
            def _():
                coef_copy(tile, me).start()

        return carry

    lax.fori_loop(0, blocks, first_pass, 0)
    faces[gx, blocks * gx] = jnp.zeros((24, 256), jnp.float32)
    pl.semaphore_wait(barrier, sections + 2)
    face = pltpu.make_async_remote_copy(
        src_ref=faces.at[gx, blocks * (1 - gx)], dst_ref=faces.at[gx, blocks * gx],
        send_sem=halo_ssem.at[0], recv_sem=halo_rsem.at[0],
        device_id={"gx": 1 - gx}, device_id_type=MESH,
    )
    face.start()
    high = pltpu.make_async_remote_copy(
        src_ref=ys.at[0], dst_ref=yr.at[0], send_sem=halo_ssem.at[1], recv_sem=halo_rsem.at[1],
        device_id={"gy": above}, device_id_type=MESH,
    )
    high.start()
    low = pltpu.make_async_remote_copy(
        src_ref=ys.at[1], dst_ref=yr.at[1], send_sem=halo_ssem.at[2], recv_sem=halo_rsem.at[2],
        device_id={"gy": below}, device_id_type=MESH,
    )
    low.start()
    lax.fori_loop(0, blocks, first_send, 0)
    face.wait()
    high.wait()
    low.wait()

    def second_pass(step, carry):
        block = first_block(step)
        rows = pl.ds(pl.multiple_of(8 * block, 8), 8)
        left = jnp.where(gy > 0, yr[0, rows, :], 0.0)
        right = jnp.where(gy < gy_count - 1, yr[1, rows, :], 0.0)
        for e in range(5):
            base, side = [], []
            for k in range(DEPTH):
                n = 4 * e + k
                full = base_part[n, rows, :] + jnp.where(sublane == 0, faces[0, block, n : n + 1, :], 0.0)
                incoming = jnp.where(small_lane == 0, pltpu.roll(left, (128 - n) % 128, 1), 0.0)
                base.append((tile_of(full, 0) + incoming, tile_of(full, 1)))
                full = up_part[n, rows, :] + jnp.where(sublane == 7, faces[1, block + 1, n : n + 1, :], 0.0)
                incoming = jnp.where(small_lane == 127, pltpu.roll(right, 127 - n, 1), 0.0)
                side.append((tile_of(full, 0), tile_of(full, 1) + incoming))
            for h in range(2):
                tile = 2 * block + h
                f = [gain[tile, k] for k in range(DEPTH)]
                b = [gain[tile, 4 + k] for k in range(DEPTH)]
                if CLASS[e] != 2:
                    s = [gain[tile, 8 + k] for k in range(DEPTH)]
                    sign = 1.0 if CLASS[e] == 0 else -1.0
                    f = [x + sign * y for x, y in zip(f, s)]
                    b = [x - sign * y for x, y in zip(b, s)]
                lower = [base[0][h]]
                for k in range(1, DEPTH):
                    lower.append(base[k][h] + f[k - 1] * lower[k - 1])
                term_out[tile, e] = f[3] * lower[3]
                upper = lower[3] - side[3][h]
                part[tile, 4 * e + 3] = upper
                for k in (2, 1, 0):
                    upper = lower[k] - side[k][h] + b[k + 1] * upper
                    part[tile, 4 * e + k] = upper
                term_out[tile, 5 + e] = b[0] * upper
        for h in range(2):
            tile = 2 * block + h

            @pl.when(tile != me)
            def _():
                term_copy(tile, me).start()

        return carry

    lax.fori_loop(0, blocks, second_pass, 0)

    for j in range(NCOEF):
        coef_in[me, j] = coef_out[me, j]
    for j in range(NTERM):
        term_in[me, j] = term_out[me, j]

    def await_parts(step, carry):
        other = lax.rem(me + step, sections)
        coef_copy(other, other).wait_recv()
        term_copy(other, other).wait_recv()
        return carry

    lax.fori_loop(1, sections, await_parts, 0)

    zero = jnp.zeros((8, 128), jnp.float32)

    def go_up(section, carry):
        nxt = []
        for e in range(5):
            link_out[section, e] = carry[e]
            nxt.append(coef_in[section, CLASS[e]] * carry[e] + term_in[section, e])
        return tuple(nxt)

    lax.fori_loop(0, sections, go_up, (zero,) * 5)

    def go_down(step, carry):
        section = sections - 1 - step
        nxt = []
        for e in range(5):
            link_out[section, 5 + e] = carry[e]
            nxt.append(
                coef_in[section, 3 + CLASS[e]] * carry[e]
                + (term_in[section, 5 + e] + coef_in[section, 6 + CLASS[e]] * link_out[section, e])
            )
        return tuple(nxt)

    lax.fori_loop(0, sections, go_down, (zero,) * 5)

    def give_back(step, carry):
        link_copy(lax.rem(me + step, sections), me).start()
        return carry

    lax.fori_loop(1, sections, give_back, 0)
    for j in range(NTERM):
        link_in[me, j] = link_out[me, j]

    def store_copy(tile):
        rows = pl.ds(pl.multiple_of(8 * (tile // 2), 8), 8)
        columns = pl.ds(pl.multiple_of(128 * lax.rem(tile, 2), 128), 128)
        return pltpu.make_async_copy(
            result.at[tile], out_hbm.at[:, :, rows, columns], store_sem.at[tile]
        )

    def last_pass(step, carry):
        tile = lax.rem(me - step + sections, sections)

        @pl.when(step > 0)
        def _():
            link_copy(tile, tile).wait_recv()

        for k in range(DEPTH):
            value = []
            for e in range(5):
                c = CLASS[e]
                v = part[tile, 4 * e + k] + pull[tile, 4 * c + k] * link_in[tile, e]
                if k < 3:
                    v = v + pull[tile, 12 + 3 * c + k] * link_in[tile, 5 + e]
                else:
                    v = v + link_in[tile, 5 + e]
                value.append(v)
            rdiag = scale[tile, k]
            mean = 0.25 * (value[0] + value[1])
            halfway = 0.5 * value[2]
            result[tile, 0, k] = (mean + halfway) * rdiag
            result[tile, 1, k] = value[3] * rdiag
            result[tile, 2, k] = value[4] * rdiag
            result[tile, 3, k] = (0.5 / ROOT2) * (value[0] - value[1]) * rdiag
            result[tile, 4, k] = (mean - halfway) * rdiag
        store_copy(tile).start()
        return carry

    lax.fori_loop(0, sections, last_pass, 0)

    def finish(step, carry):
        other = lax.rem(me + step, sections)
        coef_copy(other, other).wait_send()
        term_copy(other, other).wait_send()
        link_copy(other, other).wait_send()
        return carry

    lax.fori_loop(1, sections, finish, 0)

    def drain(tile, carry):
        store_copy(tile).wait()
        return carry

    lax.fori_loop(0, sections, drain, 0)


def per_device(sections, gy_count, conserved, residual):
    rows, columns = conserved.shape[2], conserved.shape[3]
    blocks = rows // 8
    f32 = jnp.float32
    vmem = lambda *shape: pltpu.VMEM(shape, f32)
    dma = pltpu.SemaphoreType.DMA
    return pl.pallas_call(
        functools.partial(sweep_kernel, sections, gy_count, blocks),
        out_shape=jax.ShapeDtypeStruct(conserved.shape, f32),
        in_specs=[pl.BlockSpec(memory_space=pl.ANY)] * 2,
        out_specs=pl.BlockSpec(memory_space=pl.ANY),
        scratch_shapes=[
            vmem(*conserved.shape),
            vmem(*residual.shape),
            vmem(sections, 12, 8, 128),
            vmem(20, rows, columns),
            vmem(20, rows, columns),
            vmem(2, blocks + 1, 24, columns),
            vmem(sections, 21, 8, 128),
            vmem(sections, 20, 8, 128),
            vmem(sections, 4, 8, 128),
            vmem(sections, NCOEF, 8, 128),
            vmem(sections, NCOEF, 8, 128),
            vmem(sections, NTERM, 8, 128),
            vmem(sections, NTERM, 8, 128),
            vmem(sections, NTERM, 8, 128),
            vmem(sections, NTERM, 8, 128),
            vmem(2, rows, 128),
            vmem(2, rows, 128),
            vmem(sections, 5, 4, 8, 128),
            dma((2, blocks)),
            dma((sections,)),
            dma((sections,)),
            dma((sections,)),
            dma((sections,)),
            dma((sections,)),
            dma((sections,)),
            dma((3,)),
            dma((3,)),
            dma((sections,)),
        ],
        compiler_params=pltpu.CompilerParams(
            collective_id=0, has_side_effects=True, vmem_limit_bytes=48 << 20
        ),
    )(conserved, residual)


def solution(mesh):
    spec = P(None, "gz", "gx", "gy")
    return jax.shard_map(
        functools.partial(per_device, mesh.shape["gz"], mesh.shape["gy"]),
        mesh=mesh, in_specs=(spec, spec), out_specs=spec, check_vma=False,
    )
```

time: 461 us -> 40.1 us (0.09)
  the two profiles are of different devices: /device:TPU:118 before, /device:TPU:1 now
where the time goes in v1:
time: 40.1 us; the launch traced here: 39.9 us
  Pallas kernels  36.2 us (90%)
  local copies, waits for them, and re-layouts  3.69 us (9%)
    pallas_call x1, Pallas kernels, per_device(): pl.pallas_call(functools.partial(sweep_kernel, sections, gy_count, blocks...  36.2 us
    unnamed x5, local copies, waits for them, and re-layouts  3.69 us

profile of v1, /device:TPU:1, one launch (start us, length us, event | category | flops | bytes accessed | tf_op | source)
XLA Modules:
  0.0 39.9 jit_solution(10591617920354678014)
XLA Ops:
  0.0 0.0 copy-start
  0.0 1.3 %copy-done = f32[5,4,64,256]{3,2,1,0:T(8,128)S(1)} copy-done((f32[5,4,64,256]{3,2,1,0:T(8,128)S(1)}, f32[5,4,64,256]{3,2,1,0:T(8,128)}, u32[]{:S(2)}) %copy-start) | copy-done | bytes 1310744
  1.3 0.0 copy-start.1
  1.3 1.3 %copy-done.1 = f32[5,4,64,256]{3,2,1,0:T(8,128)S(1)} copy-done((f32[5,4,64,256]{3,2,1,0:T(8,128)S(1)}, f32[5,4,64,256]{3,2,1,0:T(8,128)}, u32[]{:S(2)}) %copy-start.1) | copy-done | bytes 1310744
  2.6 36.2 %shard_map.28 = f32[5,4,64,256]{3,2,1,0:T(8,128)S(1)} custom-call(f32[5,4,64,256]{3,2,1,0:T(8,128)S(1)} %copy-done, f32[5,4,64,256]{3,2,1,0:T(8,128)S(1)} %copy-done.1), custom_call_target="tpu_custom_call" | custom-call | tf_op jit(solution)/shard_map/pallas_call | solution.py:383
  38.9 1.1 %copy.4 = f32[5,4,64,256]{3,2,1,0:T(8,128)} copy(f32[5,4,64,256]{3,2,1,0:T(8,128)S(1)} %shard_map.28) | data formatting | bytes 2621440
Async XLA Ops:
  0.0 1.3 %copy-start = (f32[5,4,64,256]{3,2,1,0:T(8,128)S(1)}, f32[5,4,64,256]{3,2,1,0:T(8,128)}, u32[]{:S(2)}) copy-start(f32[5,4,64,256]{3,2,1,0:T(8,128)} %cons_hbm.1) | copy-start | bytes 3932164
  1.3 1.3 %copy-start.1 = (f32[5,4,64,256]{3,2,1,0:T(8,128)S(1)}, f32[5,4,64,256]{3,2,1,0:T(8,128)}, u32[]{:S(2)}) copy-start(f32[5,4,64,256]{3,2,1,0:T(8,128)} %res_hbm.1) | copy-start | bytes 3932164

commit v2 on v1

--- a/solution.py
+++ b/solution.py
@@ -17,6 +17,9 @@
 DEPTH = 4
 NCOEF = 9
 NTERM = 10
+GROUPS = ((2, 3, 4), (0, 1))
+START = (0, 6)
+SIZE = (6, 4)
 
 
 def tile_of(value, half):
@@ -25,12 +28,12 @@
 
 def sweep_kernel(
     sections, gy_count, blocks,
-    cons_hbm, res_hbm, out_hbm,
+    cons_hbm, res_hbm, out,
     cons, res, gain, base_part, up_part, faces, pull, part, scale,
     coef_out, coef_in, term_out, term_in, link_out, link_in,
-    ys, yr, result,
+    ys, yr,
     load_sem, coef_ssem, coef_rsem, term_ssem, term_rsem, link_ssem, link_rsem,
-    halo_ssem, halo_rsem, store_sem,
+    halo_ssem, halo_rsem,
 ):
     me = lax.axis_index("gz")
     gx = lax.axis_index("gx")
@@ -79,17 +82,19 @@
             device_id={"gz": tile}, device_id_type=MESH,
         )
 
-    def term_copy(tile, slot):
+    def term_copy(group, tile, slot):
+        span = pl.ds(START[group], SIZE[group])
         return pltpu.make_async_remote_copy(
-            src_ref=term_out.at[tile], dst_ref=term_in.at[slot],
-            send_sem=term_ssem.at[tile], recv_sem=term_rsem.at[slot],
+            src_ref=term_out.at[tile, span], dst_ref=term_in.at[slot, span],
+            send_sem=term_ssem.at[group, tile], recv_sem=term_rsem.at[group, slot],
             device_id={"gz": tile}, device_id_type=MESH,
         )
 
-    def link_copy(section, slot):
+    def link_copy(group, section, slot):
+        span = pl.ds(START[group], SIZE[group])
         return pltpu.make_async_remote_copy(
-            src_ref=link_out.at[section], dst_ref=link_in.at[slot],
-            send_sem=link_ssem.at[section], recv_sem=link_rsem.at[slot],
+            src_ref=link_out.at[section, span], dst_ref=link_in.at[slot, span],
+            send_sem=link_ssem.at[group, section], recv_sem=link_rsem.at[group, slot],
             device_id={"gz": section}, device_id_type=MESH,
         )
 
@@ -231,12 +236,12 @@
     high.wait()
     low.wait()
 
-    def second_pass(step, carry):
+    def second_pass(group, step, carry):
         block = first_block(step)
         rows = pl.ds(pl.multiple_of(8 * block, 8), 8)
         left = jnp.where(gy > 0, yr[0, rows, :], 0.0)
         right = jnp.where(gy < gy_count - 1, yr[1, rows, :], 0.0)
-        for e in range(5):
+        for place, e in enumerate(GROUPS[group]):
             base, side = [], []
             for k in range(DEPTH):
                 n = 4 * e + k
@@ -258,102 +263,107 @@
                 lower = [base[0][h]]
                 for k in range(1, DEPTH):
                     lower.append(base[k][h] + f[k - 1] * lower[k - 1])
-                term_out[tile, e] = f[3] * lower[3]
+                term_out[tile, START[group] + place] = f[3] * lower[3]
                 upper = lower[3] - side[3][h]
                 part[tile, 4 * e + 3] = upper
                 for k in (2, 1, 0):
                     upper = lower[k] - side[k][h] + b[k + 1] * upper
                     part[tile, 4 * e + k] = upper
-                term_out[tile, 5 + e] = b[0] * upper
+                term_out[tile, START[group] + SIZE[group] // 2 + place] = b[0] * upper
         for h in range(2):
             tile = 2 * block + h
 
             @pl.when(tile != me)
             def _():
-                term_copy(tile, me).start()
-
-        return carry
-
-    lax.fori_loop(0, blocks, second_pass, 0)
+                term_copy(group, tile, me).start()
+
+        return carry
+
+    for group in range(2):
+        lax.fori_loop(0, blocks, functools.partial(second_pass, group), 0)
 
     for j in range(NCOEF):
         coef_in[me, j] = coef_out[me, j]
     for j in range(NTERM):
         term_in[me, j] = term_out[me, j]
 
-    def await_parts(step, carry):
+    def await_coefs(step, carry):
         other = lax.rem(me + step, sections)
         coef_copy(other, other).wait_recv()
-        term_copy(other, other).wait_recv()
-        return carry
-
-    lax.fori_loop(1, sections, await_parts, 0)
-
-    zero = jnp.zeros((8, 128), jnp.float32)
-
-    def go_up(section, carry):
+        return carry
+
+    def await_terms(group, step, carry):
+        other = lax.rem(me + step, sections)
+        term_copy(group, other, other).wait_recv()
+        return carry
+
+    def go_up(group, section, carry):
         nxt = []
-        for e in range(5):
-            link_out[section, e] = carry[e]
-            nxt.append(coef_in[section, CLASS[e]] * carry[e] + term_in[section, e])
+        for place, e in enumerate(GROUPS[group]):
+            j = START[group] + place
+            link_out[section, j] = carry[place]
+            nxt.append(coef_in[section, CLASS[e]] * carry[place] + term_in[section, j])
         return tuple(nxt)
 
-    lax.fori_loop(0, sections, go_up, (zero,) * 5)
-
-    def go_down(step, carry):
+    def go_down(group, step, carry):
         section = sections - 1 - step
         nxt = []
-        for e in range(5):
-            link_out[section, 5 + e] = carry[e]
+        for place, e in enumerate(GROUPS[group]):
+            low = START[group] + place
+            high = low + SIZE[group] // 2
+            link_out[section, high] = carry[place]
             nxt.append(
-                coef_in[section, 3 + CLASS[e]] * carry[e]
-                + (term_in[section, 5 + e] + coef_in[section, 6 + CLASS[e]] * link_out[section, e])
+                coef_in[section, 3 + CLASS[e]] * carry[place]
+                + (term_in[section, high] + coef_in[section, 6 + CLASS[e]] * link_out[section, low])
             )
         return tuple(nxt)
 
-    lax.fori_loop(0, sections, go_down, (zero,) * 5)
-
-    def give_back(step, carry):
-        link_copy(lax.rem(me + step, sections), me).start()
-        return carry
-
-    lax.fori_loop(1, sections, give_back, 0)
+    def give_back(group, step, carry):
+        link_copy(group, lax.rem(me + step, sections), me).start()
+        return carry
+
+    lax.fori_loop(1, sections, await_coefs, 0)
+    zero = jnp.zeros((8, 128), jnp.float32)
+    for group in range(2):
+        count = len(GROUPS[group])
+        lax.fori_loop(1, sections, functools.partial(await_terms, group), 0)
+        lax.fori_loop(0, sections, functools.partial(go_up, group), (zero,) * count)
+        lax.fori_loop(0, sections, functools.partial(go_down, group), (zero,) * count)
+        lax.fori_loop(1, sections, functools.partial(give_back, group), 0)
     for j in range(NTERM):
         link_in[me, j] = link_out[me, j]
 
-    def store_copy(tile):
+    def last_pass(step, carry):
+        tile = lax.rem(me - step + sections, sections)
         rows = pl.ds(pl.multiple_of(8 * (tile // 2), 8), 8)
         columns = pl.ds(pl.multiple_of(128 * lax.rem(tile, 2), 128), 128)
-        return pltpu.make_async_copy(
-            result.at[tile], out_hbm.at[:, :, rows, columns], store_sem.at[tile]
-        )
-
-    def last_pass(step, carry):
-        tile = lax.rem(me - step + sections, sections)
 
         @pl.when(step > 0)
         def _():
-            link_copy(tile, tile).wait_recv()
+            link_copy(0, tile, tile).wait_recv()
+            link_copy(1, tile, tile).wait_recv()
 
         for k in range(DEPTH):
             value = []
             for e in range(5):
                 c = CLASS[e]
-                v = part[tile, 4 * e + k] + pull[tile, 4 * c + k] * link_in[tile, e]
+                group = 0 if c == 2 else 1
+                low = START[group] + GROUPS[group].index(e)
+                high = low + SIZE[group] // 2
+                v = part[tile, 4 * e + k] + pull[tile, 4 * c + k] * link_in[tile, low]
                 if k < 3:
-                    v = v + pull[tile, 12 + 3 * c + k] * link_in[tile, 5 + e]
+                    v = v + pull[tile, 12 + 3 * c + k] * link_in[tile, high]
                 else:
-                    v = v + link_in[tile, 5 + e]
+                    v = v + link_in[tile, high]
                 value.append(v)
             rdiag = scale[tile, k]
             mean = 0.25 * (value[0] + value[1])
             halfway = 0.5 * value[2]
-            result[tile, 0, k] = (mean + halfway) * rdiag
-            result[tile, 1, k] = value[3] * rdiag
-            result[tile, 2, k] = value[4] * rdiag
-            result[tile, 3, k] = (0.5 / ROOT2) * (value[0] - value[1]) * rdiag
-            result[tile, 4, k] = (mean - halfway) * rdiag
-        store_copy(tile).start()
+            out[0, k, rows, columns] = (mean + halfway) * rdiag
+            out[1, k, rows, columns] = value[3] * rdiag
+            out[2, k, rows, columns] = value[4] * rdiag
+            out[3, k, rows, columns] = (0.5 / ROOT2) * (value[0] - value[1]) * rdiag
+            out[4, k, rows, columns] = (mean - halfway) * rdiag
         return carry
 
     lax.fori_loop(0, sections, last_pass, 0)
@@ -361,17 +371,12 @@
     def finish(step, carry):
         other = lax.rem(me + step, sections)
         coef_copy(other, other).wait_send()
-        term_copy(other, other).wait_send()
-        link_copy(other, other).wait_send()
+        for group in range(2):
+            term_copy(group, other, other).wait_send()
+            link_copy(group, other, other).wait_send()
         return carry
 
     lax.fori_loop(1, sections, finish, 0)
-
-    def drain(tile, carry):
-        store_copy(tile).wait()
-        return carry
-
-    lax.fori_loop(0, sections, drain, 0)
 
 
 def per_device(sections, gy_count, conserved, residual):
@@ -382,9 +387,9 @@
     dma = pltpu.SemaphoreType.DMA
     return pl.pallas_call(
         functools.partial(sweep_kernel, sections, gy_count, blocks),
-        out_shape=jax.ShapeDtypeStruct(conserved.shape, f32),
-        in_specs=[pl.BlockSpec(memory_space=pl.ANY)] * 2,
-        out_specs=pl.BlockSpec(memory_space=pl.ANY),
+        out_shape=pltpu.VMEM(conserved.shape, f32),
+        in_specs=[pl.BlockSpec(memory_space=pltpu.HBM)] * 2,
+        out_specs=pl.BlockSpec(memory_space=pltpu.VMEM),
         scratch_shapes=[
             vmem(*conserved.shape),
             vmem(*residual.shape),
@@ -403,20 +408,18 @@
             vmem(sections, NTERM, 8, 128),
             vmem(2, rows, 128),
             vmem(2, rows, 128),
-            vmem(sections, 5, 4, 8, 128),
             dma((2, blocks)),
             dma((sections,)),
             dma((sections,)),
-            dma((sections,)),
-            dma((sections,)),
-            dma((sections,)),
-            dma((sections,)),
+            dma((2, sections)),
+            dma((2, sections)),
+            dma((2, sections)),
+            dma((2, sections)),
             dma((3,)),
             dma((3,)),
-            dma((sections,)),
         ],
         compiler_params=pltpu.CompilerParams(
-            collective_id=0, has_side_effects=True, vmem_limit_bytes=48 << 20
+            collective_id=0, has_side_effects=True, vmem_limit_bytes=54 << 20
         ),
     )(conserved, residual)
 

time: 40.1 us -> 36.3 us (0.905)
  local copies, waits for them, and re-layouts: 3.69 us -> 1.06 us
  Pallas kernels: 36.2 us -> 35.2 us
    unnamed x5 -> x1, local copies, waits for them, and re-layouts: 3.69 us -> 1.06 us
    pallas_call x1, Pallas kernels: 36.2 us -> 35.2 us  [per_device(): pl.pallas_call(functools.partial(sweep_kernel, sections, gy_count, blocks...]
where the time goes in v2:
time: 36.3 us; the launch traced here: 36.2 us
  Pallas kernels  35.2 us (97%)
  local copies, waits for them, and re-layouts  1.06 us (3%)
    pallas_call x1, Pallas kernels, per_device(): pl.pallas_call(functools.partial(sweep_kernel, sections, gy_count, blocks...  35.2 us
    unnamed x1, local copies, waits for them, and re-layouts  1.06 us

profile of v2, /device:TPU:1, one launch (start us, length us, event | category | flops | bytes accessed | tf_op | source)
XLA Modules:
  0.0 36.2 jit_solution(7018693532552800617)
XLA Ops:
  0.0 35.2 %shard_map.28 = f32[5,4,64,256]{3,2,1,0:T(8,128)S(1)} custom-call(f32[5,4,64,256]{3,2,1,0:T(8,128)} %cons_hbm.1, f32[5,4,64,256]{3,2,1,0:T(8,128)} %res_hbm.1), custom_call_target="tpu_custom_call" | custom-call | tf_op jit(solution)/shard_map/pallas_call | solution.py:388
  35.2 1.1 %copy.4 = f32[5,4,64,256]{3,2,1,0:T(8,128)} copy(f32[5,4,64,256]{3,2,1,0:T(8,128)S(1)} %shard_map.28) | data formatting | bytes 2621440

commit v3 on v2

--- a/solution.py
+++ b/solution.py
@@ -33,7 +33,7 @@
     coef_out, coef_in, term_out, term_in, link_out, link_in,
     ys, yr,
     load_sem, coef_ssem, coef_rsem, term_ssem, term_rsem, link_ssem, link_rsem,
-    halo_ssem, halo_rsem,
+    halo_ssem, halo_rsem, plane_sem, near_sem,
 ):
     me = lax.axis_index("gz")
     gx = lax.axis_index("gx")
@@ -56,20 +56,42 @@
             copy.start()
         return carry
 
-    lax.fori_loop(0, blocks, start_load, 0)
-
     barrier = pltpu.get_barrier_semaphore()
 
     def greet(step, carry):
         pl.semaphore_signal(
-            barrier, inc=1, device_id={"gz": lax.rem(me + step, sections)}, device_id_type=MESH
-        )
-        return carry
-
+            barrier, inc=1, device_id={"gz": lax.rem(me + step, sections), "gx": 1}, device_id_type=MESH
+        )
+        return carry
+
+    lax.fori_loop(0, blocks, start_load, 0)
     lax.fori_loop(1, sections, greet, 0)
-    pl.semaphore_signal(barrier, inc=1, device_id={"gx": 1 - gx}, device_id_type=MESH)
-    pl.semaphore_signal(barrier, inc=1, device_id={"gy": above}, device_id_type=MESH)
-    pl.semaphore_signal(barrier, inc=1, device_id={"gy": below}, device_id_type=MESH)
+    pl.semaphore_signal(barrier, inc=1, device_id={"gx": 0, "gy": above}, device_id_type=MESH)
+    pl.semaphore_signal(barrier, inc=1, device_id={"gx": 0, "gy": below}, device_id_type=MESH)
+
+    @pl.when(gx == 0)
+    def _():
+        pl.semaphore_signal(barrier, inc=1, device_id={"gx": 1}, device_id_type=MESH)
+
+    def await_plane():
+        @pl.when(gx == 1)
+        def _():
+            pl.semaphore_wait(barrier, 2 * sections - 1)
+            pl.semaphore_signal(plane_sem, inc=1, device_id={"gx": 0}, device_id_type=MESH)
+
+        @pl.when(gx == 0)
+        def _():
+            pl.semaphore_wait(plane_sem, 1)
+
+    def await_neighbours():
+        @pl.when(gx == 0)
+        def _():
+            pl.semaphore_wait(barrier, 4)
+            pl.semaphore_signal(near_sem, inc=1, device_id={"gx": 1}, device_id_type=MESH)
+
+        @pl.when(gx == 1)
+        def _():
+            pl.semaphore_wait(near_sem, 1)
 
     lane = lax.broadcasted_iota(jnp.int32, (8, 256), 1)
     sublane = lax.broadcasted_iota(jnp.int32, (8, 256), 0)
@@ -77,8 +99,7 @@
 
     def coef_copy(tile, slot):
         return pltpu.make_async_remote_copy(
-            src_ref=coef_out.at[tile], dst_ref=coef_in.at[slot],
-            send_sem=coef_ssem.at[tile], recv_sem=coef_rsem.at[slot],
+            src_ref=coef_out.at[tile], dst_ref=coef_in.at[slot], send_sem=coef_ssem, recv_sem=coef_rsem,
             device_id={"gz": tile}, device_id_type=MESH,
         )
 
@@ -86,7 +107,7 @@
         span = pl.ds(START[group], SIZE[group])
         return pltpu.make_async_remote_copy(
             src_ref=term_out.at[tile, span], dst_ref=term_in.at[slot, span],
-            send_sem=term_ssem.at[group, tile], recv_sem=term_rsem.at[group, slot],
+            send_sem=term_ssem.at[group], recv_sem=term_rsem.at[group],
             device_id={"gz": tile}, device_id_type=MESH,
         )
 
@@ -94,8 +115,32 @@
         span = pl.ds(START[group], SIZE[group])
         return pltpu.make_async_remote_copy(
             src_ref=link_out.at[section, span], dst_ref=link_in.at[slot, span],
-            send_sem=link_ssem.at[group, section], recv_sem=link_rsem.at[group, slot],
+            send_sem=link_ssem.at[group], recv_sem=link_rsem.at[group, slot],
             device_id={"gz": section}, device_id_type=MESH,
+        )
+
+    others = pl.ds(0, sections - 1)
+
+    def coef_all():
+        return pltpu.make_async_remote_copy(
+            src_ref=coef_out.at[others], dst_ref=coef_in.at[others], send_sem=coef_ssem, recv_sem=coef_rsem,
+            device_id={"gz": me}, device_id_type=MESH,
+        )
+
+    def term_all(group):
+        span = pl.ds(START[group], SIZE[group])
+        return pltpu.make_async_remote_copy(
+            src_ref=term_out.at[others, span], dst_ref=term_in.at[others, span],
+            send_sem=term_ssem.at[group], recv_sem=term_rsem.at[group],
+            device_id={"gz": me}, device_id_type=MESH,
+        )
+
+    def link_sent(group):
+        span = pl.ds(START[group], SIZE[group])
+        return pltpu.make_async_remote_copy(
+            src_ref=link_out.at[others, span], dst_ref=link_in.at[others, span],
+            send_sem=link_ssem.at[group], recv_sem=link_rsem.at[group, 0],
+            device_id={"gz": me}, device_id_type=MESH,
         )
 
     def first_pass(step, carry):
@@ -199,10 +244,7 @@
             for j in range(NCOEF):
                 coef_out[2 * block + h, j] = tile_of(coefs[j], h)
 
-        return carry
-
-    def first_send(step, carry):
-        block = first_block(step)
+        pl.when(step == 0)(await_plane)
         for h in range(2):
             tile = 2 * block + h
 
@@ -214,7 +256,7 @@
 
     lax.fori_loop(0, blocks, first_pass, 0)
     faces[gx, blocks * gx] = jnp.zeros((24, 256), jnp.float32)
-    pl.semaphore_wait(barrier, sections + 2)
+    await_neighbours()
     face = pltpu.make_async_remote_copy(
         src_ref=faces.at[gx, blocks * (1 - gx)], dst_ref=faces.at[gx, blocks * gx],
         send_sem=halo_ssem.at[0], recv_sem=halo_rsem.at[0],
@@ -231,7 +273,6 @@
         device_id={"gy": below}, device_id_type=MESH,
     )
     low.start()
-    lax.fori_loop(0, blocks, first_send, 0)
     face.wait()
     high.wait()
     low.wait()
@@ -287,16 +328,6 @@
     for j in range(NTERM):
         term_in[me, j] = term_out[me, j]
 
-    def await_coefs(step, carry):
-        other = lax.rem(me + step, sections)
-        coef_copy(other, other).wait_recv()
-        return carry
-
-    def await_terms(group, step, carry):
-        other = lax.rem(me + step, sections)
-        term_copy(group, other, other).wait_recv()
-        return carry
-
     def go_up(group, section, carry):
         nxt = []
         for place, e in enumerate(GROUPS[group]):
@@ -322,16 +353,19 @@
         link_copy(group, lax.rem(me + step, sections), me).start()
         return carry
 
-    lax.fori_loop(1, sections, await_coefs, 0)
+    coef_all().wait_recv()
     zero = jnp.zeros((8, 128), jnp.float32)
     for group in range(2):
         count = len(GROUPS[group])
-        lax.fori_loop(1, sections, functools.partial(await_terms, group), 0)
-        lax.fori_loop(0, sections, functools.partial(go_up, group), (zero,) * count)
-        lax.fori_loop(0, sections, functools.partial(go_down, group), (zero,) * count)
+        term_all(group).wait_recv()
+        lax.fori_loop(0, sections, functools.partial(go_up, group), (zero,) * count, unroll=True)
+        lax.fori_loop(0, sections, functools.partial(go_down, group), (zero,) * count, unroll=True)
         lax.fori_loop(1, sections, functools.partial(give_back, group), 0)
     for j in range(NTERM):
         link_in[me, j] = link_out[me, j]
+    coef_all().wait_send()
+    for group in range(2):
+        term_all(group).wait_send()
 
     def last_pass(step, carry):
         tile = lax.rem(me - step + sections, sections)
@@ -368,15 +402,8 @@
 
     lax.fori_loop(0, sections, last_pass, 0)
 
-    def finish(step, carry):
-        other = lax.rem(me + step, sections)
-        coef_copy(other, other).wait_send()
-        for group in range(2):
-            term_copy(group, other, other).wait_send()
-            link_copy(group, other, other).wait_send()
-        return carry
-
-    lax.fori_loop(1, sections, finish, 0)
+    for group in range(2):
+        link_sent(group).wait_send()
 
 
 def per_device(sections, gy_count, conserved, residual):
@@ -409,14 +436,16 @@
             vmem(2, rows, 128),
             vmem(2, rows, 128),
             dma((2, blocks)),
-            dma((sections,)),
-            dma((sections,)),
-            dma((2, sections)),
-            dma((2, sections)),
-            dma((2, sections)),
+            dma(()),
+            dma(()),
+            dma((2,)),
+            dma((2,)),
+            dma((2,)),
             dma((2, sections)),
             dma((3,)),
             dma((3,)),
+            pltpu.SemaphoreType.REGULAR,
+            pltpu.SemaphoreType.REGULAR,
         ],
         compiler_params=pltpu.CompilerParams(
             collective_id=0, has_side_effects=True, vmem_limit_bytes=54 << 20

time: 36.3 us -> 34.5 us (0.950); the launches traced: 36.2 us -> 33.9 us
  Pallas kernels: 35.2 us -> 32.8 us
    pallas_call x1, Pallas kernels: 35.2 us -> 32.8 us  [per_device(): pl.pallas_call(functools.partial(sweep_kernel, sections, gy_count, blocks...]
where the time goes in v3:
time: 34.5 us; the launch traced here: 33.9 us
  Pallas kernels  32.8 us (95%)
  local copies, waits for them, and re-layouts  1.06 us (3%)
    pallas_call x1, Pallas kernels, per_device(): pl.pallas_call(functools.partial(sweep_kernel, sections, gy_count, blocks...  32.8 us
    unnamed x1, local copies, waits for them, and re-layouts  1.06 us

profile of v3, /device:TPU:1, one launch (start us, length us, event | category | flops | bytes accessed | tf_op | source)
XLA Modules:
  0.0 33.9 jit_solution(10184638502088078366)
XLA Ops:
  0.0 32.8 %shard_map.28 = f32[5,4,64,256]{3,2,1,0:T(8,128)S(1)} custom-call(f32[5,4,64,256]{3,2,1,0:T(8,128)} %cons_hbm.1, f32[5,4,64,256]{3,2,1,0:T(8,128)} %res_hbm.1), custom_call_target="tpu_custom_call" | custom-call | tf_op jit(solution)/shard_map/pallas_call | solution.py:415
  32.8 1.1 %copy.4 = f32[5,4,64,256]{3,2,1,0:T(8,128)} copy(f32[5,4,64,256]{3,2,1,0:T(8,128)S(1)} %shard_map.28) | data formatting | bytes 2621440

commit v4 on v3

--- a/solution.py
+++ b/solution.py
@@ -142,6 +142,16 @@
             send_sem=link_ssem.at[group], recv_sem=link_rsem.at[group, 0],
             device_id={"gz": me}, device_id_type=MESH,
         )
+
+    def first_send(step, carry):
+        for h in range(2):
+            tile = 2 * first_block(step) + h
+
+            @pl.when(tile != me)
+            def _():
+                coef_copy(tile, me).start()
+
+        return carry
 
     def first_pass(step, carry):
         block = first_block(step)
@@ -244,13 +254,14 @@
             for j in range(NCOEF):
                 coef_out[2 * block + h, j] = tile_of(coefs[j], h)
 
-        pl.when(step == 0)(await_plane)
-        for h in range(2):
-            tile = 2 * block + h
-
-            @pl.when(tile != me)
-            def _():
-                coef_copy(tile, me).start()
+        @pl.when(step == 4)
+        def _():
+            await_plane()
+            lax.fori_loop(0, step, first_send, 0)
+
+        @pl.when(step >= 4)
+        def _():
+            first_send(step, 0)
 
         return carry
 

time: 34.5 us -> 33.4 us (0.968)
  Pallas kernels: 32.8 us -> 31.7 us
    pallas_call x1, Pallas kernels: 32.8 us -> 31.7 us  [per_device(): pl.pallas_call(functools.partial(sweep_kernel, sections, gy_count, blocks...]
where the time goes in v4:
time: 33.4 us; the launch traced here: 32.8 us
  Pallas kernels  31.7 us (95%)
  local copies, waits for them, and re-layouts  1.06 us (3%)
    pallas_call x1, Pallas kernels, per_device(): pl.pallas_call(functools.partial(sweep_kernel, sections, gy_count, blocks...  31.7 us
    unnamed x1, local copies, waits for them, and re-layouts  1.06 us

profile of v4, /device:TPU:1, one launch (start us, length us, event | category | flops | bytes accessed | tf_op | source)
XLA Modules:
  0.0 32.8 jit_solution(1993281709350865283)
XLA Ops:
  0.0 31.7 %shard_map.28 = f32[5,4,64,256]{3,2,1,0:T(8,128)S(1)} custom-call(f32[5,4,64,256]{3,2,1,0:T(8,128)} %cons_hbm.1, f32[5,4,64,256]{3,2,1,0:T(8,128)} %res_hbm.1), custom_call_target="tpu_custom_call" | custom-call | tf_op jit(solution)/shard_map/pallas_call | solution.py:426
  31.7 1.1 %copy.4 = f32[5,4,64,256]{3,2,1,0:T(8,128)} copy(f32[5,4,64,256]{3,2,1,0:T(8,128)S(1)} %shard_map.28) | data formatting | bytes 2621440

commit v5 on v4

--- a/solution.py
+++ b/solution.py
@@ -64,7 +64,6 @@
         )
         return carry
 
-    lax.fori_loop(0, blocks, start_load, 0)
     lax.fori_loop(1, sections, greet, 0)
     pl.semaphore_signal(barrier, inc=1, device_id={"gx": 0, "gy": above}, device_id_type=MESH)
     pl.semaphore_signal(barrier, inc=1, device_id={"gx": 0, "gy": below}, device_id_type=MESH)
@@ -73,6 +72,8 @@
     def _():
         pl.semaphore_signal(barrier, inc=1, device_id={"gx": 1}, device_id_type=MESH)
 
+    lax.fori_loop(0, blocks, start_load, 0)
+
     def await_plane():
         @pl.when(gx == 1)
         def _():
@@ -147,7 +148,7 @@
         for h in range(2):
             tile = 2 * first_block(step) + h
 
-            @pl.when(tile != me)
+            @pl.when((tile != me) & ((step > 0) | (tile > me)))
             def _():
                 coef_copy(tile, me).start()
 
@@ -254,18 +255,25 @@
             for j in range(NCOEF):
                 coef_out[2 * block + h, j] = tile_of(coefs[j], h)
 
-        @pl.when(step == 4)
+        @pl.when(step == 5)
         def _():
             await_plane()
             lax.fori_loop(0, step, first_send, 0)
 
-        @pl.when(step >= 4)
+        @pl.when(step >= 5)
         def _():
             first_send(step, 0)
 
         return carry
 
     lax.fori_loop(0, blocks, first_pass, 0)
+
+    odd = lax.rem(me, 2)
+
+    @pl.when(odd == 1)
+    def _():
+        coef_copy(me - 1, me).start()
+
     faces[gx, blocks * gx] = jnp.zeros((24, 256), jnp.float32)
     await_neighbours()
     face = pltpu.make_async_remote_copy(
@@ -325,7 +333,7 @@
         for h in range(2):
             tile = 2 * block + h
 
-            @pl.when(tile != me)
+            @pl.when((tile != me) & ((step > 0) | (tile > me)))
             def _():
                 term_copy(group, tile, me).start()
 
@@ -333,6 +341,11 @@
 
     for group in range(2):
         lax.fori_loop(0, blocks, functools.partial(second_pass, group), 0)
+
+        @pl.when(odd == 1)
+        def _():
+            term_copy(group, me - 1, me).start()
+
 
     for j in range(NCOEF):
         coef_in[me, j] = coef_out[me, j]

time: 33.4 us -> 33.2 us (level)
  no operation moved by 1% of the time
where the time goes in v5:
time: 33.2 us; the launch traced here: 32.8 us
  Pallas kernels  31.7 us (95%)
  local copies, waits for them, and re-layouts  1.06 us (3%)
    pallas_call x1, Pallas kernels, per_device(): pl.pallas_call(functools.partial(sweep_kernel, sections, gy_count, blocks...  31.7 us
    unnamed x1, local copies, waits for them, and re-layouts  1.06 us

profile of v5, /device:TPU:1, one launch (start us, length us, event | category | flops | bytes accessed | tf_op | source)
XLA Modules:
  0.0 32.8 jit_solution(2789754202644267306)
XLA Ops:
  0.0 31.7 %shard_map.28 = f32[5,4,64,256]{3,2,1,0:T(8,128)S(1)} custom-call(f32[5,4,64,256]{3,2,1,0:T(8,128)} %cons_hbm.1, f32[5,4,64,256]{3,2,1,0:T(8,128)} %res_hbm.1), custom_call_target="tpu_custom_call" | custom-call | tf_op jit(solution)/shard_map/pallas_call | solution.py:439
  31.7 1.1 %copy.4 = f32[5,4,64,256]{3,2,1,0:T(8,128)} copy(f32[5,4,64,256]{3,2,1,0:T(8,128)S(1)} %shard_map.28) | data formatting | bytes 2621440

commit v6 on v5

--- a/solution.py
+++ b/solution.py
@@ -391,40 +391,43 @@
     for group in range(2):
         term_all(group).wait_send()
 
-    def last_pass(step, carry):
+    def solved(tile, k, e):
+        c = CLASS[e]
+        group = 0 if c == 2 else 1
+        low = START[group] + GROUPS[group].index(e)
+        high = low + SIZE[group] // 2
+        v = part[tile, 4 * e + k] + pull[tile, 4 * c + k] * link_in[tile, low]
+        if k < 3:
+            return v + pull[tile, 12 + 3 * c + k] * link_in[tile, high]
+        return v + link_in[tile, high]
+
+    def last_pass(group, step, carry):
         tile = lax.rem(me - step + sections, sections)
         rows = pl.ds(pl.multiple_of(8 * (tile // 2), 8), 8)
         columns = pl.ds(pl.multiple_of(128 * lax.rem(tile, 2), 128), 128)
 
         @pl.when(step > 0)
         def _():
-            link_copy(0, tile, tile).wait_recv()
-            link_copy(1, tile, tile).wait_recv()
+            link_copy(group, tile, tile).wait_recv()
 
         for k in range(DEPTH):
-            value = []
-            for e in range(5):
-                c = CLASS[e]
-                group = 0 if c == 2 else 1
-                low = START[group] + GROUPS[group].index(e)
-                high = low + SIZE[group] // 2
-                v = part[tile, 4 * e + k] + pull[tile, 4 * c + k] * link_in[tile, low]
-                if k < 3:
-                    v = v + pull[tile, 12 + 3 * c + k] * link_in[tile, high]
-                else:
-                    v = v + link_in[tile, high]
-                value.append(v)
             rdiag = scale[tile, k]
-            mean = 0.25 * (value[0] + value[1])
-            halfway = 0.5 * value[2]
-            out[0, k, rows, columns] = (mean + halfway) * rdiag
-            out[1, k, rows, columns] = value[3] * rdiag
-            out[2, k, rows, columns] = value[4] * rdiag
-            out[3, k, rows, columns] = (0.5 / ROOT2) * (value[0] - value[1]) * rdiag
-            out[4, k, rows, columns] = (mean - halfway) * rdiag
-        return carry
-
-    lax.fori_loop(0, sections, last_pass, 0)
+            if group == 0:
+                halfway = 0.5 * solved(tile, k, 2)
+                out[0, k, rows, columns] = halfway * rdiag
+                out[1, k, rows, columns] = solved(tile, k, 3) * rdiag
+                out[2, k, rows, columns] = solved(tile, k, 4) * rdiag
+            else:
+                p, q = solved(tile, k, 0), solved(tile, k, 1)
+                mean = 0.25 * (p + q) * rdiag
+                halfway = out[0, k, rows, columns]
+                out[0, k, rows, columns] = mean + halfway
+                out[3, k, rows, columns] = (0.5 / ROOT2) * (p - q) * rdiag
+                out[4, k, rows, columns] = mean - halfway
+        return carry
+
+    for group in range(2):
+        lax.fori_loop(0, sections, functools.partial(last_pass, group), 0)
 
     for group in range(2):
         link_sent(group).wait_send()

time: 33.2 us -> 33.1 us (level)
  no operation moved by 1% of the time
where the time goes in v6:
time: 33.1 us; the launch traced here: 32.7 us
  Pallas kernels  31.6 us (95%)
  local copies, waits for them, and re-layouts  1.06 us (3%)
    pallas_call x1, Pallas kernels, per_device(): pl.pallas_call(functools.partial(sweep_kernel, sections, gy_count, blocks...  31.6 us
    unnamed x1, local copies, waits for them, and re-layouts  1.06 us

profile of v6, /device:TPU:1, one launch (start us, length us, event | category | flops | bytes accessed | tf_op | source)
XLA Modules:
  0.0 32.7 jit_solution(7330914922715014058)
XLA Ops:
  0.0 31.6 %shard_map.28 = f32[5,4,64,256]{3,2,1,0:T(8,128)S(1)} custom-call(f32[5,4,64,256]{3,2,1,0:T(8,128)} %cons_hbm.1, f32[5,4,64,256]{3,2,1,0:T(8,128)} %res_hbm.1), custom_call_target="tpu_custom_call" | custom-call | tf_op jit(solution)/shard_map/pallas_call | solution.py:442
  31.6 1.1 %copy.4 = f32[5,4,64,256]{3,2,1,0:T(8,128)} copy(f32[5,4,64,256]{3,2,1,0:T(8,128)S(1)} %shard_map.28) | data formatting | bytes 2621440

commit v7 on v6

--- a/solution.py
+++ b/solution.py
@@ -275,13 +275,13 @@
         coef_copy(me - 1, me).start()
 
     faces[gx, blocks * gx] = jnp.zeros((24, 256), jnp.float32)
-    await_neighbours()
     face = pltpu.make_async_remote_copy(
         src_ref=faces.at[gx, blocks * (1 - gx)], dst_ref=faces.at[gx, blocks * gx],
         send_sem=halo_ssem.at[0], recv_sem=halo_rsem.at[0],
         device_id={"gx": 1 - gx}, device_id_type=MESH,
     )
     face.start()
+    await_neighbours()
     high = pltpu.make_async_remote_copy(
         src_ref=ys.at[0], dst_ref=yr.at[0], send_sem=halo_ssem.at[1], recv_sem=halo_rsem.at[1],
         device_id={"gy": above}, device_id_type=MESH,

time: 33.1 us -> 33.1 us (level)
  no operation moved by 1% of the time
where the time goes in v7:
time: 33.1 us; the launch traced here: 32.8 us
  Pallas kernels  31.7 us (96%)
  local copies, waits for them, and re-layouts  1.06 us (3%)
    pallas_call x1, Pallas kernels, per_device(): pl.pallas_call(functools.partial(sweep_kernel, sections, gy_count, blocks...  31.7 us
    unnamed x1, local copies, waits for them, and re-layouts  1.06 us

profile of v7, /device:TPU:1, one launch (start us, length us, event | category | flops | bytes accessed | tf_op | source)
XLA Modules:
  0.0 32.8 jit_solution(6368532680082725243)
XLA Ops:
  0.0 31.7 %shard_map.28 = f32[5,4,64,256]{3,2,1,0:T(8,128)S(1)} custom-call(f32[5,4,64,256]{3,2,1,0:T(8,128)} %cons_hbm.1, f32[5,4,64,256]{3,2,1,0:T(8,128)} %res_hbm.1), custom_call_target="tpu_custom_call" | custom-call | tf_op jit(solution)/shard_map/pallas_call | solution.py:442
  31.7 1.1 %copy.4 = f32[5,4,64,256]{3,2,1,0:T(8,128)} copy(f32[5,4,64,256]{3,2,1,0:T(8,128)S(1)} %shard_map.28) | data formatting | bytes 2621440
